TPU v7x, 128 devices: a whole 4x4x4 slice. The times are simulated.
128 devices in a mesh: dp: 2 (over core), expert: 32 (over x, z_hi, y), replica: 2 (over z_lo).
Axes of the slice: x: 4, y: 4, z: 4 (z_hi: 2, z_lo: 2; z = z_hi * 2 + z_lo), core: 2. Of those that a mesh axis runs over, the one named last changes fastest.
Arguments:
- tokens: bfloat16 [16384, 4096], P(('dp', 'expert', 'replica')), may hold values from -6 to 6
- expert_ids: int32 [16384, 8], P(('dp', 'expert', 'replica')), may hold values from 0 to 63, all different within a row; in each aligned block of 128 rows (0 to 127, 128 to 255, ...) at most 24 rows name the same one
- router_weight: bfloat16 [4096, 64], replicated, may hold values from -0.09375 to 0.09375
- gate_weight: bfloat16 [64, 4096, 768], P(('expert', 'replica')), may hold values from -0.09375 to 0.09375
- up_weight: bfloat16 [64, 4096, 768], P(('expert', 'replica')), may hold values from -0.09375 to 0.09375
- down_weight: bfloat16 [64, 768, 4096], P(('expert', 'replica')), may hold values from -0.21875 to 0.21875
- cotangent: bfloat16 [16384, 4096], P(('dp', 'expert', 'replica')), may hold values from -0.09375 to 0.09375
Outputs:
- mixed: bfloat16 [16384, 4096], P(('dp', 'expert', 'replica'))
- router_grad: float32 [4096, 64], replicated
Inputs may be any that keep to these rules, and one draw needn't show every extreme that they name: `expert_ids`: in each aligned block of 128 rows (the rows of one device) no expert is named by more than 24 rows, and in every draw some expert is named by exactly 24 rows of some block.
All inputs are finite; a program needn't handle non-finite values.
Results may differ from a plain program's by a relative error of at most 0.0057.
Values may be sent and summed in bfloat16 or wider, within the bound.
No kernel may reach another device: no remote copies, remote signals or barrier semaphores. Data moves between devices by JAX's collectives and lax.ppermute only.
A program may use at most 128 MiB of HBM per device.

v0:
```python
import jax
import jax.numpy as jnp
from jax import lax
from jax.sharding import PartitionSpec as P


def expert_apply(incoming, gate_mat, up_mat, down_mat):
    model_width = incoming.shape[-1]
    flat_rows = incoming.reshape(-1, model_width)
    gate_act = jnp.dot(flat_rows, gate_mat, preferred_element_type=jnp.float32)
    up_act = jnp.dot(flat_rows, up_mat, preferred_element_type=jnp.float32)
    hidden = (jax.nn.silu(gate_act) * up_act).astype(jnp.bfloat16)
    result = jnp.dot(hidden, down_mat, preferred_element_type=jnp.float32).astype(jnp.bfloat16)
    return result.reshape(incoming.shape)


def local(tokens, expert_ids, router_weight, gate_weight, up_weight, down_weight, cotangent):
    tok_rows, model_width = tokens.shape
    top_count = expert_ids.shape[1]
    experts = router_weight.shape[1]
    capacity = 3 * tok_rows * top_count // (2 * experts)
    logits = jnp.dot(tokens, router_weight, preferred_element_type=jnp.float32)
    onehot = (expert_ids[:, :, None] == jnp.arange(experts, dtype=jnp.int32)[None, None, :]).astype(
        jnp.float32
    )
    chosen = jnp.einsum("tke,te->tk", onehot, logits, precision=lax.Precision.HIGHEST)
    raised = jnp.exp(chosen)
    gate_probs = raised / jnp.sum(raised, axis=1, keepdims=True)
    flat_ids = expert_ids.reshape(-1)
    member = (flat_ids[:, None] == jnp.arange(experts, dtype=jnp.int32)[None, :]).astype(jnp.int32)
    before = jnp.cumsum(member, axis=0) - member
    slot_place = jnp.sum(before * member, axis=1)
    target = flat_ids * capacity + slot_place
    token_of_slot = jnp.arange(tok_rows * top_count, dtype=jnp.int32) // top_count
    outbox = (
        jnp.zeros((experts * capacity, model_width), jnp.bfloat16)
        .at[target]
        .set(tokens[token_of_slot])
    )
    outbox = outbox.reshape(experts, capacity, model_width)
    gate_mat = gate_weight[0]
    up_mat = up_weight[0]
    down_mat = down_weight[0]
    returned = lax.all_to_all(
        expert_apply(
            lax.all_to_all(outbox, ("expert", "replica"), split_axis=0, concat_axis=0, tiled=True),
            gate_mat,
            up_mat,
            down_mat,
        ),
        ("expert", "replica"),
        split_axis=0,
        concat_axis=0,
        tiled=True,
    )
    returned = returned.reshape(experts * capacity, model_width)
    slot_rows = returned[target].reshape(tok_rows, top_count, model_width)
    mixed = jnp.sum(gate_probs[:, :, None] * slot_rows, axis=1).astype(jnp.bfloat16)
    slot_dots = jnp.einsum("tkd,td->tk", slot_rows, cotangent, preferred_element_type=jnp.float32)
    logit_grad = gate_probs * (slot_dots - jnp.sum(gate_probs * slot_dots, axis=1, keepdims=True))
    grad_table = jnp.einsum("tk,tke->te", logit_grad, onehot, precision=lax.Precision.HIGHEST)
    local_grad = jnp.dot(tokens.astype(jnp.float32).T, grad_table, precision=lax.Precision.HIGHEST)
    router_grad = lax.psum(local_grad, ("dp", "expert", "replica"))
    return (mixed, router_grad)


def solution(mesh):
    in_specs = (
        P(("dp", "expert", "replica"), None),
        P(("dp", "expert", "replica"), None),
        P(),
        P(("expert", "replica"), None, None),
        P(("expert", "replica"), None, None),
        P(("expert", "replica"), None, None),
        P(("dp", "expert", "replica"), None),
    )
    out_specs = (P(("dp", "expert", "replica"), None), P())
    return jax.shard_map(local, mesh=mesh, in_specs=in_specs, out_specs=out_specs, check_vma=False)
```

profile of v0, /device:TPU:0, one launch (start us, length us, event | category | flops | bytes accessed | tf_op | source)
XLA Modules:
  0.0 652.7 jit_solution(2259549610414264721)
XLA Ops:
  7.2 0.0 copy-start
  7.2 0.9 copy.10
  8.1 0.1 eq.45
  8.1 0.1 eq.41
  8.2 0.7 broadcast_multiply_fusion
  9.0 18.0 %reduce-window.6 = s32[64,8,128]{2,1,0:T(8,128)S(1)} reduce-window(s32[64,8,128]{2,1,0:T(8,128)S(1)} %fusion.19, s32[]{:T(128)} %constant.29.clone.1), window={size=1x1x128 pad=0_0x0_0x127_0}, to_apply=%region_1.0 | reduce-window | flops 8323072 | bytes 524292 | tf_op jit(solution)/shard_map/reduce-window
  27.0 0.1 slice.12
  27.1 0.1 copy.14
  27.3 0.1 copy.15
  27.4 0.1 broadcast_add_fusion
  27.5 0.1 copy.11
  27.6 0.1 mul.43
  27.7 0.1 fusion.16
  27.8 0.0 copy-done
  27.8 7.8 %gather_fusion = bf16[1024,4096]{1,0:T(8,128)(2,1)} fusion(bf16[128,4096]{1,0:T(8,128)(2,1)S(1)} %copy-done, s32[1024]{0:T(1024)S(1)} %broadcast_clamp_fusion.1), kind=kCustom, calls=%fused_computation | custom fusion | bytes 16781312 | tf_op jit(solution)/shard_map/gather | solution.py:38
  35.6 20.0 %scatter_custom_fusion = bf16[1536,4096]{1,0:T(8,128)(2,1)} fusion(s32[1024]{0:T(1024)S(1)} %bitcast.78, bf16[1024,4096]{1,0:T(8,128)(2,1)} %gather_fusion, bf16[]{:T(256)} %constant.27.clone.1), kind=kCustom, calls=%fused_computation.12 | custom fusion | bytes 12583424 | tf_op jit(solution)/shard_map/scatter | solution.py:38
  55.7 0.0 slice-start
  55.7 160.1 %all_to_all.10 = bf16[64,24,4096]{2,1,0:T(8,128)(2,1)S(1)} all-to-all(bf16[64,24,4096]{2,1,0:T(8,128)(2,1)} %bitcast.64), channel_id=1, replica_groups=mesh['dp'=2,'expert'=32,'replica'=2] {'expert','replica'}, dimensions={0} | all-to-all | bytes 25165824 | tf_op jit(solution)/shard_map/all_to_all | solution.py:46
  215.8 0.0 slice-start.1
  215.8 13.3 %fusion.3 = f32[1536,768]{1,0:T(8,128)} fusion(bf16[1536,4096]{1,0:T(8,128)(2,1)S(1)} %bitcast.66, bf16[1,4096,768]{2,1,0:T(8,128)(2,1)} %param.11), kind=kOutput, calls=%fused_computation.8 | convolution fusion | flops 9663676416 | bytes 23592960 | tf_op jit(solution)/shard_map/dot_general | solution.py:11
  229.1 0.0 slice-done
  229.1 0.0 slice-done.1
  229.1 12.2 %multiply_convert_fusion = bf16[1536,768]{1,0:T(8,128)(2,1)S(1)} fusion(f32[1536,768]{1,0:T(8,128)} %fusion.3, bf16[1536,4096]{1,0:T(8,128)(2,1)S(1)} %bitcast.67, bf16[1,4096,768]{2,1,0:T(8,128)(2,1)S(1)} %bitcast.82), kind=kOutput, calls=%fused_computation.14 | convolution fusion | flops 9670754304 | bytes 25952256 | tf_op jit(solution)/shard_map/dot_general | solution.py:10
  241.3 15.1 %convolution_convert_fusion = bf16[1536,4096]{1,0:T(8,128)(2,1)} fusion(bf16[1536,768]{1,0:T(8,128)(2,1)S(1)} %multiply_convert_fusion, bf16[1,768,4096]{2,1,0:T(8,128)(2,1)} %param.12), kind=kOutput, calls=%fused_computation.4 | convolution fusion | flops 9669967872 | bytes 21233664 | tf_op jit(solution)/shard_map/dot_general | solution.py:13
  256.4 0.0 copy-start.1
  256.4 5.9 all-to-all-start.1
  262.3 0.3 all-reduce.2.cloned.1.call-start
  262.5 0.0 copy-done.1
  262.6 0.4 fusion.20
  263.0 0.6 fusion.13
  263.6 0.1 exponential_reduce_fusion
  263.7 175.0 %all-to-all-done.1 = bf16[64,24,4096]{2,1,0:T(8,128)(2,1)} async-done(((bf16[64,24,4096]{2,1,0:T(8,128)(2,1)}), bf16[64,24,4096]{2,1,0:T(8,128)(2,1)}, u32[]{:S(2)}, u32[]{:S(2)}) %all-to-all-start.1) | async-done | bytes 12582944 | tf_op jit(solution)/shard_map/all_to_all | solution.py:44
  438.7 0.0 copy-start.2
  438.7 21.4 %gather_fusion.1 = bf16[1024,4096]{1,0:T(8,128)(2,1)} fusion(bf16[1536,4096]{1,0:T(8,128)(2,1)} %bitcast.15, s32[1024]{0:T(1024)S(1)} %broadcast_clamp_fusion), kind=kCustom, calls=%fused_computation.1 | custom fusion | bytes 16781312 | tf_op jit(solution)/shard_map/gather | solution.py:57
  460.1 0.0 copy-done.2
  460.1 8.9 %fusion = f32[128,1,8]{2,1,0:T(1,128)S(1)} fusion(bf16[1024,4096]{1,0:T(8,128)(2,1)} %gather_fusion.1, bf16[128,4096,1]{1,0,2:T(8,128)(2,1)S(1)} %bitcast.83), kind=kOutput, calls=%fused_computation.5 | convolution fusion | flops 8388608 | bytes 9441280 | tf_op jit(solution)/shard_map/tkd,td->tk/dot_general | solution.py:59
  468.9 0.2 multiply_reduce_fusion.1
  469.1 0.1 subtract_multiply_fusion
  469.2 0.6 fusion.12
  469.8 1.6 convolution_bitcast_fusion
  471.4 0.0 all-reduce.2.cloned.1.call-update
  471.5 12.9 %multiply_reduce_fusion = bf16[128,4096]{1,0:T(8,128)(2,1)} fusion(bf16[1024,4096]{1,0:T(8,128)(2,1)} %gather_fusion.1, f32[128,8]{1,0:T(8,128)S(1)} %get-tuple-element.3), kind=kLoop, calls=%fused_computation.3 | loop fusion | flops 12058624 | bytes 9441280 | tf_op jit(solution)/shard_map/reduce_sum | solution.py:58
  484.4 158.9 %all-reduce.2.cloned.1.call-done = f32[4096,64]{0,1:T(8,128)} async-done(((f32[4096,64]{0,1:T(8,128)}), f32[4096,64]{0,1:T(8,128)}) %all-reduce.2.cloned.1.call-update) | async-done | bytes 1048592 | tf_op jit(solution)/shard_map/psum | solution.py:63
  643.2 2.3 copy.27
  (8 shorter events, 0.1 us)
Async XLA Ops:
  7.2 20.7 %copy-start = (bf16[128,4096]{1,0:T(8,128)(2,1)S(1)}, bf16[128,4096]{1,0:T(8,128)(2,1)}, u32[]{:S(2)}) copy-start(bf16[128,4096]{1,0:T(8,128)(2,1)} %param.7) | copy-start | bytes 3145732
  55.7 173.4 %slice-start = ((s8[6291456]{0:T(1024)(128)(4,1)}), s8[4194304]{0:T(1024)(128)(4,1)S(1)}, s32[]{:S(2)}) async-start(s8[6291456]{0:T(1024)(128)(4,1)} %bitcast.81), calls=%async_computation.3 | async-start | bytes 8388608
  215.8 13.3 %slice-start.1 = ((s8[6291456]{0:T(1024)(128)(4,1)}), s8[2097152]{0:T(1024)(128)(4,1)S(1)}, s32[]{:S(2)}) async-start(s8[6291456]{0:T(1024)(128)(4,1)} %bitcast.81), calls=%async_computation.4 | async-start | bytes 4194304
  256.4 6.2 copy-start.1
  256.4 182.4 %all-to-all-start.1 = ((bf16[64,24,4096]{2,1,0:T(8,128)(2,1)}), bf16[64,24,4096]{2,1,0:T(8,128)(2,1)}, u32[]{:S(2)}, u32[]{:S(2)}) async-start(bf16[64,24,4096]{2,1,0:T(8,128)(2,1)} %bitcast.65), calls=%async_computation.1 | async-start | bytes 25165824 | tf_op jit(solution)/shard_map/all_to_all | solution.py:44
  262.3 380.9 %all-reduce.2.cloned.1.call-start = ((), (), s32[]{:S(2)}) async-start(), calls=%async_computation.2 | async-start | bytes 2097152 | tf_op jit(solution)/shard_map/psum | solution.py:63
  438.7 21.4 %copy-start.2 = (bf16[128,4096]{1,0:T(8,128)(2,1)S(1)}, bf16[128,4096]{1,0:T(8,128)(2,1)}, u32[]{:S(2)}) copy-start(bf16[128,4096]{1,0:T(8,128)(2,1)} %param.13) | copy-start | bytes 3145732
Sparse Core Ops, SparseCore 0:
  471.6 171.5 all-reduce.1
where the time goes:
time: 662 us; the launch traced here: 653 us
  waiting for transfers between devices  334 us (50%)
  blocking collectives  160 us (24%)
  local copies, waits for them, and re-layouts  53.1 us (8%)
  matrix products  52.7 us (8%)
  other arithmetic  32.3 us (5%)
  between operations  14.6 us (2%)
    all_to_all x1, waiting for transfers between devices, local(): lax.all_to_all(expert_apply(lax.all_to_all(outbox, ('expert', 'replica'),...  175 us
    all_to_all x1, blocking collectives, local(): lax.all_to_all(outbox, ('expert', 'replica'), split_axis=0, concat_axis=0...  160 us
    psum x1, waiting for transfers between devices, local(): router_grad = lax.psum(local_grad, ('dp', 'expert', 'replica'))  159 us
    gather x1, local copies, waits for them, and re-layouts, local(): slot_rows = returned[target].reshape(tok_rows, top_count, model_width)  21.4 us
    scatter x1, local copies, waits for them, and re-layouts, local(): outbox = jnp.zeros((experts * capacity, model_width), jnp.bfloat16).at[ta...  20 us
    another operation x3, other arithmetic  18.2 us
    dot_general x1, matrix products, expert_apply(): jnp.dot(hidden, down_mat, preferred_element_type=jnp.float32)  15.1 us
    dot_general x1, matrix products, expert_apply(): up_act = jnp.dot(flat_rows, up_mat, preferred_element_type=jnp.float32)  13.3 us
  transfers between devices with their start and end apart: 2, of which 2 were waited for; matrix products, arithmetic and copies ran while one was open for 2% of the time, Pallas kernels for 0%

commit v1 on v0

v1 whole, which is shorter than its diff:
```python
import jax
import jax.numpy as jnp
from jax import lax
from jax.sharding import PartitionSpec as P

GROUP = ("expert", "replica")
STEP = 8


def exchange(rows):
    return lax.all_to_all(rows, GROUP, split_axis=0, concat_axis=0, tiled=True)


def expert_apply(rows, gate_mat, up_mat, down_mat):
    gate_act = jnp.dot(rows, gate_mat, preferred_element_type=jnp.float32)
    up_act = jnp.dot(rows, up_mat, preferred_element_type=jnp.float32)
    hidden = (jax.nn.silu(gate_act) * up_act).astype(jnp.bfloat16)
    return jnp.dot(hidden, down_mat, preferred_element_type=jnp.float32).astype(jnp.bfloat16)


def local(tokens, expert_ids, router_weight, gate_weight, up_weight, down_weight, cotangent):
    tok_rows, model_width = tokens.shape
    top_count = expert_ids.shape[1]
    experts = router_weight.shape[1]
    capacity = 3 * tok_rows * top_count // (2 * experts)
    ids_t = expert_ids.T
    names = jnp.arange(experts, dtype=jnp.int32)
    member = jnp.any(ids_t[:, None, :] == names[None, :, None], axis=0)
    earlier = (jnp.arange(tok_rows)[:, None] < jnp.arange(tok_rows)[None, :]).astype(jnp.bfloat16)
    before = jnp.dot(member.astype(jnp.bfloat16), earlier, preferred_element_type=jnp.float32)
    slot = jnp.where(member, before.astype(jnp.int32), -1)

    picks = []
    sent = []
    for start in range(0, capacity, STEP):
        wanted = start + jnp.arange(STEP, dtype=jnp.int32)
        pick = (slot[:, None, :] == wanted[None, :, None]).reshape(experts * STEP, tok_rows)
        box = jnp.dot(pick.astype(jnp.bfloat16), tokens, preferred_element_type=jnp.float32)
        picks.append(pick)
        sent.append(exchange(box.astype(jnp.bfloat16).reshape(experts, STEP, model_width)))

    logits = lax.dot_general(
        router_weight, tokens, (((0,), (1,)), ((), ())), preferred_element_type=jnp.float32
    )
    raised = jnp.where(member, jnp.exp(logits), 0.0)
    probs = raised / jnp.sum(raised, axis=0, keepdims=True)

    mixed = jnp.zeros((tok_rows, model_width), jnp.float32)
    dots = jnp.zeros((experts, tok_rows), jnp.float32)
    for pick, rows in zip(picks, sent):
        out = expert_apply(rows.reshape(-1, model_width), gate_weight[0], up_weight[0], down_weight[0])
        back = exchange(out.reshape(experts, STEP, model_width)).reshape(-1, model_width)
        every = lax.dot_general(
            back, cotangent, (((1,), (1,)), ((), ())), preferred_element_type=jnp.float32
        )
        dots = dots + jnp.sum(jnp.where(pick, every, 0.0).reshape(experts, STEP, tok_rows), axis=1)
        share = jnp.where(
            pick.reshape(experts, STEP, tok_rows), probs[:, None, :], 0.0
        ).astype(jnp.bfloat16).reshape(-1, tok_rows)
        mixed = mixed + lax.dot_general(
            share, back, (((0,), (0,)), ((), ())), preferred_element_type=jnp.float32
        )
    table = probs * (dots - jnp.sum(probs * dots, axis=0, keepdims=True))
    grad = jnp.dot(table, tokens.astype(jnp.float32), precision=lax.Precision.HIGHEST)
    row = jnp.sum(exchange(grad), axis=0, keepdims=True)
    row = row + lax.ppermute(row, "dp", [(0, 1), (1, 0)])
    router_grad = exchange(jnp.broadcast_to(row, (experts, model_width)))
    return (mixed.astype(jnp.bfloat16), router_grad.T)


def solution(mesh):
    in_specs = (
        P(("dp", "expert", "replica"), None),
        P(("dp", "expert", "replica"), None),
        P(),
        P(("expert", "replica"), None, None),
        P(("expert", "replica"), None, None),
        P(("expert", "replica"), None, None),
        P(("dp", "expert", "replica"), None),
    )
    out_specs = (P(("dp", "expert", "replica"), None), P())
    return jax.shard_map(local, mesh=mesh, in_specs=in_specs, out_specs=out_specs, check_vma=False)
```

time: 662 us -> 454 us (0.69)
  blocking collectives: 160 us -> 26.5 us
  waiting for transfers between devices: 334 us -> 231 us
  matrix products: 52.7 us -> 121 us
  starting transfers between devices: 6.16 us -> 60.7 us
  local copies, waits for them, and re-layouts: 53.1 us -> 5.1 us
  other arithmetic: 32.3 us -> 1.73 us
  between operations: 14.6 us -> 1.09 us
    psum x1 -> x0, waiting for transfers between devices: 159 us -> none  [local(): router_grad = lax.psum(local_grad, ('dp', 'expert', 'replica'))]
    all_to_all x1, blocking collectives: 160 us -> 26.5 us  [exchange(): return lax.all_to_all(rows, GROUP, split_axis=0, concat_axis=0, tiled=True)]
    all_to_all x1 -> x7, waiting for transfers between devices: 175 us -> 230 us  [exchange(): return lax.all_to_all(rows, GROUP, split_axis=0, concat_axis=0, tiled=True)]
    all_to_all x1 -> x7, starting transfers between devices: 5.91 us -> 60.6 us  [exchange(): return lax.all_to_all(rows, GROUP, split_axis=0, concat_axis=0, tiled=True)]
    dot_general x1 -> x3, matrix products: 15.1 us -> 51 us  [expert_apply(): jnp.dot(hidden, down_mat, preferred_element_type=jnp.float32)]
    dot_general x7 -> x15, matrix products: 37.6 us -> 69.6 us  [the longest x3 25.9 us: expert_apply(): gate_act = jnp.dot(rows, gate_mat, preferred_element_type=jnp.float32)]
    gather x2 -> x0, local copies, waits for them, and re-layouts: 29.2 us -> none  [the longest x1 21.4 us: local(): slot_rows = returned[target].reshape(tok_rows, top_count, model_width)]
    scatter x1 -> x0, local copies, waits for them, and re-layouts: 20 us -> none  [local(): outbox = jnp.zeros((experts * capacity, model_width), jnp.bfloat16).at[ta...]
  transfers between devices with their start and end apart: 2 -> 8, of which waited for: 2 -> 7; matrix products, arithmetic and copies ran while one was open for 2% -> 25% of each run, Pallas kernels for 0% -> 0%
where the time goes in v1:
time: 454 us; the launch traced here: 447 us
  waiting for transfers between devices  231 us (51%)
  matrix products  121 us (27%)
  starting transfers between devices  60.7 us (13%)
  blocking collectives  26.5 us (6%)
  local copies, waits for them, and re-layouts  5.1 us (1%)
    all_to_all x7, waiting for transfers between devices, exchange(): return lax.all_to_all(rows, GROUP, split_axis=0, concat_axis=0, tiled=True)  230 us
    all_to_all x7, starting transfers between devices, exchange(): return lax.all_to_all(rows, GROUP, split_axis=0, concat_axis=0, tiled=True)  60.6 us
    dot_general x3, matrix products, expert_apply(): jnp.dot(hidden, down_mat, preferred_element_type=jnp.float32)  51 us
    all_to_all x1, blocking collectives, exchange(): return lax.all_to_all(rows, GROUP, split_axis=0, concat_axis=0, tiled=True)  26.5 us
    dot_general x3, matrix products, expert_apply(): gate_act = jnp.dot(rows, gate_mat, preferred_element_type=jnp.float32)  25.9 us
    dot_general x3, matrix products, local(): lax.dot_general(share, back, (((0,), (0,)), ((), ())), preferred_element_...  22.4 us
    dot_general x3, matrix products, local(): lax.dot_general(back, cotangent, (((1,), (1,)), ((), ())), preferred_elem...  10.4 us
    dot_general x3, matrix products, local(): jnp.dot(pick.astype(jnp.bfloat16), tokens, preferred_element_type=jnp.flo...  9.75 us
  transfers between devices with their start and end apart: 8, of which 7 were waited for; matrix products, arithmetic and copies ran while one was open for 25% of the time, Pallas kernels for 0%

profile of v1, /device:TPU:0, one launch (start us, length us, event | category | flops | bytes accessed | tf_op | source)
XLA Modules:
  0.0 446.7 jit_solution(16173228468659287895)
XLA Ops:
  0.6 0.0 copy-start
  0.7 0.8 fusion.113
  1.5 0.1 fusion.109
  1.6 0.1 eq.91
  1.7 0.2 copy-done
  1.9 3.3 fusion.37
  5.1 11.8 %all-to-all-start.2 = ((bf16[64,8,4096]{2,1,0:T(8,128)(2,1)}), bf16[64,8,4096]{2,1,0:T(8,128)(2,1)}, u32[]{:S(2)}, u32[]{:S(2)}) async-start(bf16[64,8,4096]{2,1,0:T(8,128)(2,1)} %fusion.37), calls=%async_computation.2 | async-start | bytes 8388608 | tf_op jit(solution)/shard_map/all_to_all | solution.py:11
  17.0 0.1 eq.97
  17.1 3.2 fusion.38
  20.3 50.1 %all-to-all-done.2 = bf16[64,8,4096]{2,1,0:T(8,128)(2,1)} async-done(((bf16[64,8,4096]{2,1,0:T(8,128)(2,1)}), bf16[64,8,4096]{2,1,0:T(8,128)(2,1)}, u32[]{:S(2)}, u32[]{:S(2)}) %all-to-all-start.2) | async-done | bytes 4194336 | tf_op jit(solution)/shard_map/all_to_all | solution.py:11
  70.4 7.9 %all-to-all-start.4 = ((bf16[64,8,4096]{2,1,0:T(8,128)(2,1)}), bf16[64,8,4096]{2,1,0:T(8,128)(2,1)}, u32[]{:S(2)}, u32[]{:S(2)}) async-start(bf16[64,8,4096]{2,1,0:T(8,128)(2,1)} %fusion.38), calls=%async_computation.4 | async-start | bytes 8388608 | tf_op jit(solution)/shard_map/all_to_all | solution.py:11
  78.3 0.1 eq.85
  78.4 3.3 fusion.36
  81.7 50.2 %all-to-all-done.4 = bf16[64,8,4096]{2,1,0:T(8,128)(2,1)} async-done(((bf16[64,8,4096]{2,1,0:T(8,128)(2,1)}), bf16[64,8,4096]{2,1,0:T(8,128)(2,1)}, u32[]{:S(2)}, u32[]{:S(2)}) %all-to-all-start.4) | async-done | bytes 4194336 | tf_op jit(solution)/shard_map/all_to_all | solution.py:11
  131.9 8.7 %all-to-all-start = ((bf16[64,8,4096]{2,1,0:T(8,128)(2,1)}), bf16[64,8,4096]{2,1,0:T(8,128)(2,1)}, u32[]{:S(2)}, u32[]{:S(2)}) async-start(bf16[64,8,4096]{2,1,0:T(8,128)(2,1)} %fusion.36), calls=%async_computation | async-start | bytes 8388608 | tf_op jit(solution)/shard_map/all_to_all | solution.py:11
  140.6 8.7 %fusion.14 = f32[512,768]{1,0:T(8,128)} fusion(bf16[1,4096,768]{2,1,0:T(8,128)(2,1)} %param.10, bf16[64,8,4096]{2,1,0:T(8,128)(2,1)} %all-to-all-done.2), kind=kOutput, calls=%fused_computation.14 | convolution fusion | flops 3221225472 | bytes 12058624 | tf_op jit(solution)/shard_map/dot_general | solution.py:15
  149.2 17.0 %fusion.30 = bf16[64,8,4096]{2,1,0:T(8,128)(2,1)} fusion(bf16[1,768,4096]{2,1,0:T(8,128)(2,1)} %param.12, f32[512,768]{1,0:T(8,128)} %fusion.14, bf16[1,4096,768]{2,1,0:T(8,128)(2,1)} %param.11, bf16[64,8,4096]{2,1,0:T(8,128)(2,1)} %all-to-all-done.2), kind=kOutput, calls=%fused_computation.25 | convolution fusion | flops 6446907392 | bytes 22544384 | tf_op jit(solution)/shard_map/dot_general | solution.py:18
  166.2 27.9 %all-to-all-done = bf16[64,8,4096]{2,1,0:T(8,128)(2,1)} async-done(((bf16[64,8,4096]{2,1,0:T(8,128)(2,1)}), bf16[64,8,4096]{2,1,0:T(8,128)(2,1)}, u32[]{:S(2)}, u32[]{:S(2)}) %all-to-all-start) | async-done | bytes 4194336 | tf_op jit(solution)/shard_map/all_to_all | solution.py:11
  194.1 9.5 %all-to-all-start.3 = ((bf16[64,8,4096]{2,1,0:T(8,128)(2,1)}), bf16[64,8,4096]{2,1,0:T(8,128)(2,1)}, u32[]{:S(2)}, u32[]{:S(2)}) async-start(bf16[64,8,4096]{2,1,0:T(8,128)(2,1)} %fusion.30), calls=%async_computation.3 | async-start | bytes 8388608 | tf_op jit(solution)/shard_map/all_to_all | solution.py:11
  203.6 8.6 %fusion.12 = f32[512,768]{1,0:T(8,128)} fusion(bf16[1,4096,768]{2,1,0:T(8,128)(2,1)} %param.10, bf16[64,8,4096]{2,1,0:T(8,128)(2,1)} %all-to-all-done.4), kind=kOutput, calls=%fused_computation.12 | convolution fusion | flops 3221225472 | bytes 12058624 | tf_op jit(solution)/shard_map/dot_general | solution.py:15
  212.3 17.0 %fusion.27 = bf16[64,8,4096]{2,1,0:T(8,128)(2,1)} fusion(bf16[1,768,4096]{2,1,0:T(8,128)(2,1)} %param.12, f32[512,768]{1,0:T(8,128)} %fusion.12, bf16[1,4096,768]{2,1,0:T(8,128)(2,1)} %param.11, bf16[64,8,4096]{2,1,0:T(8,128)(2,1)} %all-to-all-done.4), kind=kOutput, calls=%fused_computation.24 | convolution fusion | flops 6446907392 | bytes 22544384 | tf_op jit(solution)/shard_map/dot_general | solution.py:18
  229.3 27.8 %all-to-all-done.3 = bf16[64,8,4096]{2,1,0:T(8,128)(2,1)} async-done(((bf16[64,8,4096]{2,1,0:T(8,128)(2,1)}), bf16[64,8,4096]{2,1,0:T(8,128)(2,1)}, u32[]{:S(2)}, u32[]{:S(2)}) %all-to-all-start.3) | async-done | bytes 4194336 | tf_op jit(solution)/shard_map/all_to_all | solution.py:11
  257.1 8.4 %all-to-all-start.5 = ((bf16[64,8,4096]{2,1,0:T(8,128)(2,1)}), bf16[64,8,4096]{2,1,0:T(8,128)(2,1)}, u32[]{:S(2)}, u32[]{:S(2)}) async-start(bf16[64,8,4096]{2,1,0:T(8,128)(2,1)} %fusion.27), calls=%async_computation.5 | async-start | bytes 8388608 | tf_op jit(solution)/shard_map/all_to_all | solution.py:11
  265.4 8.7 %fusion.16 = f32[512,768]{1,0:T(8,128)} fusion(bf16[1,4096,768]{2,1,0:T(8,128)(2,1)} %param.10, bf16[64,8,4096]{2,1,0:T(8,128)(2,1)} %all-to-all-done), kind=kOutput, calls=%fused_computation.16 | convolution fusion | flops 3221225472 | bytes 12058624 | tf_op jit(solution)/shard_map/dot_general | solution.py:15
  274.1 17.0 %fusion.33 = bf16[64,8,4096]{2,1,0:T(8,128)(2,1)} fusion(bf16[1,768,4096]{2,1,0:T(8,128)(2,1)} %param.12, f32[512,768]{1,0:T(8,128)} %fusion.16, bf16[1,4096,768]{2,1,0:T(8,128)(2,1)} %param.11, bf16[64,8,4096]{2,1,0:T(8,128)(2,1)} %all-to-all-done), kind=kOutput, calls=%fused_computation.26 | convolution fusion | flops 6446907392 | bytes 22544384 | tf_op jit(solution)/shard_map/dot_general | solution.py:18
  291.1 0.0 copy-start.1
  291.1 0.0 copy-start.2
  291.1 27.9 %all-to-all-done.5 = bf16[64,8,4096]{2,1,0:T(8,128)(2,1)} async-done(((bf16[64,8,4096]{2,1,0:T(8,128)(2,1)}), bf16[64,8,4096]{2,1,0:T(8,128)(2,1)}, u32[]{:S(2)}, u32[]{:S(2)}) %all-to-all-start.5) | async-done | bytes 4194336 | tf_op jit(solution)/shard_map/all_to_all | solution.py:11
  318.9 9.5 %all-to-all-start.1 = ((bf16[64,8,4096]{2,1,0:T(8,128)(2,1)}), bf16[64,8,4096]{2,1,0:T(8,128)(2,1)}, u32[]{:S(2)}, u32[]{:S(2)}) async-start(bf16[64,8,4096]{2,1,0:T(8,128)(2,1)} %fusion.33), calls=%async_computation.1 | async-start | bytes 8388608 | tf_op jit(solution)/shard_map/all_to_all | solution.py:11
  328.4 0.0 copy-done.1
  328.5 0.5 fusion.140
  329.0 0.0 copy-done.2
  329.0 3.5 fusion.102
  332.4 3.5 fusion.99
  335.9 46.0 %all-to-all-done.1 = bf16[64,8,4096]{2,1,0:T(8,128)(2,1)} async-done(((bf16[64,8,4096]{2,1,0:T(8,128)(2,1)}), bf16[64,8,4096]{2,1,0:T(8,128)(2,1)}, u32[]{:S(2)}, u32[]{:S(2)}) %all-to-all-start.1) | async-done | bytes 4194336 | tf_op jit(solution)/shard_map/all_to_all | solution.py:11
  381.9 3.5 fusion.105
  385.4 0.6 convolution_bitcast_fusion.3
  386.0 1.1 copy.29
  387.0 26.5 %all_to_all.48 = f32[64,1,4096]{2,1,0:T(1,128)S(1)} all-to-all(f32[64,1,4096]{2,1,0:T(1,128)S(1)} %copy.29), channel_id=1, replica_groups=mesh['dp'=2,'expert'=32,'replica'=2] {'expert','replica'}, dimensions={0} | all-to-all | bytes 2097152 | tf_op jit(solution)/shard_map/all_to_all | solution.py:11
  413.5 0.9 reduce_sum.59
  414.4 0.1 collective-permute-start
  414.5 1.2 collective-permute-done
  415.7 2.0 broadcast_in_dim.63
  417.6 4.9 %all-to-all-start.7 = ((f32[64,1,4096]{2,1,0:T(1,128)}), f32[64,1,4096]{2,1,0:T(1,128)S(1)}, u32[]{:S(2)}, u32[]{:S(2)}) async-start(f32[64,1,4096]{2,1,0:T(1,128)} %broadcast_in_dim.63), calls=%async_computation.7 | async-start | bytes 2097152 | tf_op jit(solution)/shard_map/all_to_all | solution.py:11
  422.5 7.0 %convolution_bitcast_fusion.1 = f32[128,4096]{1,0:T(8,128)S(1)} fusion(bf16[64,8,4096]{2,1,0:T(8,128)(2,1)} %all-to-all-done.3, f32[64,128]{1,0:T(8,128)S(1)} %get-tuple-element.3, s32[64,128]{1,0:T(8,128)S(1)} %fusion.109, s32[8]{0:T(128)S(1)} %iota_add_fusion.1), kind=kOutput, calls=%fused_computation.31 | convolution fusion | flops 537001984 | bytes 6357024 | tf_op jit(solution)/shard_map/dot_general | solution.py:60
  429.5 7.0 %convolution_bitcast_fusion = f32[128,4096]{1,0:T(8,128)S(1)} fusion(bf16[64,8,4096]{2,1,0:T(8,128)(2,1)} %all-to-all-done.5, f32[64,128]{1,0:T(8,128)S(1)} %get-tuple-element.3, s32[64,128]{1,0:T(8,128)S(1)} %fusion.109, s32[8]{0:T(128)S(1)} %iota_add_fusion), kind=kOutput, calls=%fused_computation.30 | convolution fusion | flops 537001984 | bytes 6357024 | tf_op jit(solution)/shard_map/dot_general | solution.py:60
  436.6 8.3 %fusion.41 = bf16[128,4096]{1,0:T(8,128)(2,1)} fusion(f32[128,4096]{1,0:T(8,128)S(1)} %convolution_bitcast_fusion, f32[128,4096]{1,0:T(8,128)S(1)} %convolution_bitcast_fusion.1, bf16[64,8,4096]{2,1,0:T(8,128)(2,1)} %all-to-all-done.1, f32[64,128]{1,0:T(8,128)S(1)} %get-tuple-element.3, s32[64,128]{1,0:T(8,128)S(1)} %fusion.109), kind=kOutput, calls=%fused_computation.35 | convolution fusion | flops 538574848 | bytes 9502720 | tf_op jit(solution)/shard_map/dot_general | solution.py:60
  444.9 0.0 all-to-all-done.7
  444.9 1.6 copy.39
  (7 shorter events, 0.1 us)
Async XLA Ops:
  0.6 1.2 copy-start
  5.1 65.2 %all-to-all-start.2 = ((bf16[64,8,4096]{2,1,0:T(8,128)(2,1)}), bf16[64,8,4096]{2,1,0:T(8,128)(2,1)}, u32[]{:S(2)}, u32[]{:S(2)}) async-start(bf16[64,8,4096]{2,1,0:T(8,128)(2,1)} %fusion.37), calls=%async_computation.2 | async-start | bytes 8388608 | tf_op jit(solution)/shard_map/all_to_all | solution.py:11
  70.4 61.5 %all-to-all-start.4 = ((bf16[64,8,4096]{2,1,0:T(8,128)(2,1)}), bf16[64,8,4096]{2,1,0:T(8,128)(2,1)}, u32[]{:S(2)}, u32[]{:S(2)}) async-start(bf16[64,8,4096]{2,1,0:T(8,128)(2,1)} %fusion.38), calls=%async_computation.4 | async-start | bytes 8388608 | tf_op jit(solution)/shard_map/all_to_all | solution.py:11
  131.9 62.2 %all-to-all-start = ((bf16[64,8,4096]{2,1,0:T(8,128)(2,1)}), bf16[64,8,4096]{2,1,0:T(8,128)(2,1)}, u32[]{:S(2)}, u32[]{:S(2)}) async-start(bf16[64,8,4096]{2,1,0:T(8,128)(2,1)} %fusion.36), calls=%async_computation | async-start | bytes 8388608 | tf_op jit(solution)/shard_map/all_to_all | solution.py:11
  194.1 63.0 %all-to-all-start.3 = ((bf16[64,8,4096]{2,1,0:T(8,128)(2,1)}), bf16[64,8,4096]{2,1,0:T(8,128)(2,1)}, u32[]{:S(2)}, u32[]{:S(2)}) async-start(bf16[64,8,4096]{2,1,0:T(8,128)(2,1)} %fusion.30), calls=%async_computation.3 | async-start | bytes 8388608 | tf_op jit(solution)/shard_map/all_to_all | solution.py:11
  257.1 61.9 %all-to-all-start.5 = ((bf16[64,8,4096]{2,1,0:T(8,128)(2,1)}), bf16[64,8,4096]{2,1,0:T(8,128)(2,1)}, u32[]{:S(2)}, u32[]{:S(2)}) async-start(bf16[64,8,4096]{2,1,0:T(8,128)(2,1)} %fusion.27), calls=%async_computation.5 | async-start | bytes 8388608 | tf_op jit(solution)/shard_map/all_to_all | solution.py:11
  291.1 37.4 %copy-start.1 = (bf16[4096,64]{0,1:T(8,128)(2,1)S(1)}, bf16[4096,64]{0,1:T(8,128)(2,1)}, u32[]{:S(2)}) copy-start(bf16[4096,64]{0,1:T(8,128)(2,1)} %param.9) | copy-start | bytes 1572868
  291.1 37.9 %copy-start.2 = (bf16[128,4096]{1,0:T(8,128)(2,1)S(1)}, bf16[128,4096]{1,0:T(8,128)(2,1)}, u32[]{:S(2)}) copy-start(bf16[128,4096]{1,0:T(8,128)(2,1)} %param.13) | copy-start | bytes 3145732
  318.9 62.9 %all-to-all-start.1 = ((bf16[64,8,4096]{2,1,0:T(8,128)(2,1)}), bf16[64,8,4096]{2,1,0:T(8,128)(2,1)}, u32[]{:S(2)}, u32[]{:S(2)}) async-start(bf16[64,8,4096]{2,1,0:T(8,128)(2,1)} %fusion.33), calls=%async_computation.1 | async-start | bytes 8388608 | tf_op jit(solution)/shard_map/all_to_all | solution.py:11
  414.4 1.3 collective-permute-start
  417.6 27.2 %all-to-all-start.7 = ((f32[64,1,4096]{2,1,0:T(1,128)}), f32[64,1,4096]{2,1,0:T(1,128)S(1)}, u32[]{:S(2)}, u32[]{:S(2)}) async-start(f32[64,1,4096]{2,1,0:T(1,128)} %broadcast_in_dim.63), calls=%async_computation.7 | async-start | bytes 2097152 | tf_op jit(solution)/shard_map/all_to_all | solution.py:11

commit v2 on v1

v2 whole, which is shorter than its diff:
```python
import jax
import jax.numpy as jnp
from jax import lax
from jax.sharding import PartitionSpec as P

GROUP = ("expert", "replica")


def exchange(rows):
    return lax.all_to_all(rows, GROUP, split_axis=0, concat_axis=0, tiled=True)


def expert_apply(rows, gate_mat, up_mat, down_mat):
    gate_act = jnp.dot(rows, gate_mat, preferred_element_type=jnp.float32)
    up_act = jnp.dot(rows, up_mat, preferred_element_type=jnp.float32)
    hidden = (jax.nn.silu(gate_act) * up_act).astype(jnp.bfloat16)
    return jnp.dot(hidden, down_mat, preferred_element_type=jnp.float32).astype(jnp.bfloat16)


def local(tokens, expert_ids, router_weight, gate_weight, up_weight, down_weight, cotangent):
    tok_rows, model_width = tokens.shape
    top_count = expert_ids.shape[1]
    experts = router_weight.shape[1]
    capacity = 3 * tok_rows * top_count // (2 * experts)
    ids_t = expert_ids.T
    names = jnp.arange(experts, dtype=jnp.int32)
    member = jnp.any(ids_t[:, None, :] == names[None, :, None], axis=0)
    earlier = (jnp.arange(tok_rows)[:, None] < jnp.arange(tok_rows)[None, :]).astype(jnp.bfloat16)
    before = jnp.dot(member.astype(jnp.bfloat16), earlier, preferred_element_type=jnp.float32)
    slot = jnp.where(member, before.astype(jnp.int32), -1)

    wanted = jnp.arange(capacity, dtype=jnp.int32)
    pick = slot[:, None, :] == wanted[None, :, None]
    logits = lax.dot_general(
        router_weight, tokens, (((0,), (1,)), ((), ())), preferred_element_type=jnp.float32
    )
    raised = jnp.where(member, jnp.exp(logits), 0.0)
    probs = raised / jnp.sum(raised, axis=0, keepdims=True)
    box = jnp.dot(
        pick.reshape(-1, tok_rows).astype(jnp.bfloat16), tokens, preferred_element_type=jnp.float32
    ).astype(jnp.bfloat16)
    box, probs, slot = lax.optimization_barrier((box, probs, slot))

    rows = exchange(box.reshape(experts, capacity, model_width)).reshape(-1, model_width)
    out = expert_apply(rows, gate_weight[0], up_weight[0], down_weight[0])
    back = exchange(out.reshape(experts, capacity, model_width)).reshape(-1, model_width)

    pick = slot[:, None, :] == wanted[None, :, None]
    every = lax.dot_general(
        back, cotangent, (((1,), (1,)), ((), ())), preferred_element_type=jnp.float32
    ).reshape(experts, capacity, tok_rows)
    dots = jnp.sum(jnp.where(pick, every, 0.0), axis=1)
    table = probs * (dots - jnp.sum(probs * dots, axis=0, keepdims=True))
    slot_grad = jnp.sum(jnp.where(pick, table[:, None, :], 0.0), axis=2)
    theirs = exchange(slot_grad[:, None, :])
    share = jnp.where(pick, probs[:, None, :], 0.0).astype(jnp.bfloat16).reshape(-1, tok_rows)
    mixed = lax.dot_general(
        share, back, (((0,), (0,)), ((), ())), preferred_element_type=jnp.float32
    ).astype(jnp.bfloat16)
    row = jnp.sum(rows.astype(jnp.float32) * theirs.reshape(-1, 1), axis=0, keepdims=True)
    row = row + lax.ppermute(row, "dp", [(0, 1), (1, 0)])
    columns = exchange(jnp.broadcast_to(row.astype(jnp.bfloat16), (experts, model_width)))
    return (mixed, columns.astype(jnp.float32).T)


def solution(mesh):
    in_specs = (
        P(("dp", "expert", "replica"), None),
        P(("dp", "expert", "replica"), None),
        P(),
        P(("expert", "replica"), None, None),
        P(("expert", "replica"), None, None),
        P(("expert", "replica"), None, None),
        P(("dp", "expert", "replica"), None),
    )
    out_specs = (P(("dp", "expert", "replica"), None), P())
    return jax.shard_map(local, mesh=mesh, in_specs=in_specs, out_specs=out_specs, check_vma=False)
```

time: 454 us -> 423 us (0.932); the launches traced: 447 us -> 423 us
  blocking collectives: 26.5 us -> 326 us
  waiting for transfers between devices: 231 us -> 7.3 us
  matrix products: 121 us -> 59.6 us
  starting transfers between devices: 60.7 us -> 4.99 us
  other arithmetic: 1.73 us -> 13.2 us
  local copies, waits for them, and re-layouts: 5.1 us -> 10.4 us
    all_to_all x1 -> x3, blocking collectives: 26.5 us -> 326 us  [exchange(): return lax.all_to_all(rows, GROUP, split_axis=0, concat_axis=0, tiled=True)]
    all_to_all x7 -> x1, waiting for transfers between devices: 230 us -> 6.13 us  [exchange(): return lax.all_to_all(rows, GROUP, split_axis=0, concat_axis=0, tiled=True)]
    all_to_all x7 -> x1, starting transfers between devices: 60.6 us -> 4.9 us  [exchange(): return lax.all_to_all(rows, GROUP, split_axis=0, concat_axis=0, tiled=True)]
    dot_general x3 -> x1, matrix products: 51 us -> 12.8 us  [expert_apply(): jnp.dot(hidden, down_mat, preferred_element_type=jnp.float32)]
    dot_general x3 -> x1, matrix products: 22.4 us -> 7.47 us  [local(): lax.dot_general(share, back, (((0,), (0,)), ((), ())), preferred_element_...]
    dot_general x3 -> x1, matrix products: 25.9 us -> 14.5 us  [expert_apply(): gate_act = jnp.dot(rows, gate_mat, preferred_element_type=jnp.float32)]
    dot_general x4 -> x2, matrix products: 10.3 us -> 19.3 us  [the longest x1 15.7 us: expert_apply(): up_act = jnp.dot(rows, up_mat, preferred_element_type=jnp.float32)]
    reduce_sum x1 -> x2, other arithmetic: 0.86 us -> 8.27 us  [the longest x1 7.96 us: local(): jnp.sum(rows.astype(jnp.float32) * theirs.reshape(-1, 1), axis=0, keepdim...]
  transfers between devices with their start and end apart: 8 -> 2, of which waited for: 7 -> 2; matrix products, arithmetic and copies ran while one was open for 25% -> 2% of each run, Pallas kernels for 0% -> 0%
where the time goes in v2:
time: 423 us
  blocking collectives  326 us (77%)
  matrix products  59.6 us (14%)
  other arithmetic  13.2 us (3%)
  local copies, waits for them, and re-layouts  10.4 us (2%)
  waiting for transfers between devices  7.3 us (2%)
  starting transfers between devices  4.99 us (1%)
    all_to_all x3, blocking collectives, exchange(): return lax.all_to_all(rows, GROUP, split_axis=0, concat_axis=0, tiled=True)  326 us
    dot_general x1, matrix products, expert_apply(): up_act = jnp.dot(rows, up_mat, preferred_element_type=jnp.float32)  15.7 us
    dot_general x1, matrix products, expert_apply(): gate_act = jnp.dot(rows, gate_mat, preferred_element_type=jnp.float32)  14.5 us
    dot_general x1, matrix products, expert_apply(): jnp.dot(hidden, down_mat, preferred_element_type=jnp.float32)  12.8 us
    unnamed x18, local copies, waits for them, and re-layouts  8.68 us
  transfers between devices with their start and end apart: 2, of which 2 were waited for; matrix products, arithmetic and copies ran while one was open for 2% of the time, Pallas kernels for 0%

profile of v2, /device:TPU:0, one launch (start us, length us, event | category | flops | bytes accessed | tf_op | source)
XLA Modules:
  0.0 422.6 jit_solution(4585478636919819094)
XLA Ops:
  0.6 0.0 copy-start
  0.6 0.8 fusion.15
  1.5 0.1 fusion.10
  1.6 0.1 eq.52
  1.7 0.2 copy-done
  1.9 1.5 fusion.17
  3.4 0.3 bitcast_compare_fusion
  3.7 3.6 convolution_convert_fusion.1
  7.3 0.0 slice-start
  7.3 159.7 %all_to_all.21 = bf16[64,24,4096]{2,1,0:T(8,128)(2,1)S(1)} all-to-all(bf16[64,24,4096]{2,1,0:T(8,128)(2,1)S(1)} %bitcast.42), channel_id=1, replica_groups=mesh['dp'=2,'expert'=32,'replica'=2] {'expert','replica'}, dimensions={0} | all-to-all | bytes 25165824 | tf_op jit(solution)/shard_map/all_to_all | solution.py:10
  167.1 0.0 copy-start.3
  167.1 4.6 %copy-done.3 = bf16[64,24,4096]{2,1,0:T(8,128)(2,1)} copy-done((bf16[64,24,4096]{2,1,0:T(8,128)(2,1)}, bf16[64,24,4096]{2,1,0:T(8,128)(2,1)S(1)}, u32[]{:S(2)}) %copy-start.3) | copy-done | bytes 12582936
  171.6 0.0 slice-start.1
  171.6 15.7 %fusion.1 = f32[1536,768]{1,0:T(8,128)S(1)} fusion(bf16[1536,4096]{1,0:T(8,128)(2,1)S(1)} %bitcast.43, bf16[1,4096,768]{2,1,0:T(8,128)(2,1)} %param.11), kind=kOutput, calls=%fused_computation.4 | convolution fusion | flops 9663676416 | bytes 23592960 | tf_op jit(solution)/shard_map/dot_general | solution.py:15
  187.4 0.0 slice-done
  187.4 0.0 slice-done.1
  187.4 14.5 %multiply_convert_fusion = bf16[1536,768]{1,0:T(8,128)(2,1)} fusion(f32[1536,768]{1,0:T(8,128)S(1)} %fusion.1, bf16[1536,4096]{1,0:T(8,128)(2,1)} %bitcast.44, bf16[1,4096,768]{2,1,0:T(8,128)(2,1)S(1)} %bitcast.53), kind=kOutput, calls=%fused_computation.10 | convolution fusion | flops 9670754304 | bytes 25952256 | tf_op jit(solution)/shard_map/dot_general | solution.py:14
  201.9 12.8 %convolution_convert_fusion = bf16[1536,4096]{1,0:T(8,128)(2,1)S(1)} fusion(bf16[1536,768]{1,0:T(8,128)(2,1)} %multiply_convert_fusion, bf16[1,768,4096]{2,1,0:T(8,128)(2,1)} %param.12), kind=kOutput, calls=%fused_computation.1 | convolution fusion | flops 9669967872 | bytes 21233664 | tf_op jit(solution)/shard_map/dot_general | solution.py:17
  214.7 0.0 copy-start.4
  214.7 148.7 %all_to_all.22 = bf16[64,24,4096]{2,1,0:T(8,128)(2,1)S(1)} all-to-all(bf16[64,24,4096]{2,1,0:T(8,128)(2,1)S(1)} %bitcast.45), channel_id=1, replica_groups=mesh['dp'=2,'expert'=32,'replica'=2] {'expert','replica'}, dimensions={0} | all-to-all | bytes 25165824 | tf_op jit(solution)/shard_map/all_to_all | solution.py:10
  363.4 0.0 copy-done.4
  363.4 0.0 copy-start.2
  363.4 3.9 fusion.8
  367.3 0.6 copy-done.2
  367.9 0.3 select_reduce_fusion
  368.3 0.1 copy.24
  368.3 0.1 copy.22
  368.4 17.8 %all_to_all.23 = f32[64,1,24]{2,1,0:T(1,128)S(1)} all-to-all(f32[64,1,24]{2,1,0:T(1,128)S(1)} %copy.22), channel_id=1, replica_groups=mesh['dp'=2,'expert'=32,'replica'=2] {'expert','replica'}, dimensions={0} | all-to-all | bytes 12288 | tf_op jit(solution)/shard_map/all_to_all | solution.py:10
  386.2 8.0 %multiply_reduce_fusion = f32[4096]{0:T(1024)S(1)} fusion(bf16[64,24,4096]{2,1,0:T(8,128)(2,1)} %copy-done.3, f32[64,24]{1,0:T(8,128)S(1)} %bitcast.47), kind=kLoop, calls=%fused_computation | loop fusion | flops 18870272 | bytes 12605440 | tf_op jit(solution)/shard_map/reduce_sum | solution.py:60
  394.2 0.1 collective-permute-start
  394.3 1.2 collective-permute-done
  395.5 0.1 convert_reduce_fusion
  395.5 1.0 broadcast_in_dim.58
  396.5 0.5 broadcast.19
  397.0 3.8 reduce.3
  400.8 1.2 reshape.50
  402.0 4.9 %all-to-all-start.3 = ((bf16[64,2,2048]{2,1,0:T(2,128)(2,1)}), bf16[64,2,2048]{2,1,0:T(2,128)(2,1)S(1)}, u32[]{:S(2)}, u32[]{:S(2)}) async-start(bf16[64,2,2048]{2,1,0:T(2,128)(2,1)} %reshape.50), calls=%async_computation.3 | async-start | bytes 1048576 | tf_op jit(solution)/shard_map/all_to_all | solution.py:10
  406.9 0.0 copy-start.1
  406.9 7.5 %fusion.5 = bf16[128,4096]{1,0:T(8,128)(2,1)} fusion(bf16[64,24,4096]{2,1,0:T(8,128)(2,1)} %copy-done.2, f32[64,128]{1,0:T(8,128)S(1)} %broadcast_divide_fusion, s32[64,128]{1,0:T(8,128)S(1)} %fusion.10), kind=kOutput, calls=%fused_computation.9 | convolution fusion | flops 1611530240 | bytes 13697024 | tf_op jit(solution)/shard_map/dot_general | solution.py:57
  414.4 6.1 %all-to-all-done.3 = bf16[64,2,2048]{2,1,0:T(2,128)(2,1)S(1)} async-done(((bf16[64,2,2048]{2,1,0:T(2,128)(2,1)}), bf16[64,2,2048]{2,1,0:T(2,128)(2,1)S(1)}, u32[]{:S(2)}, u32[]{:S(2)}) %all-to-all-start.3) | async-done | bytes 524320 | tf_op jit(solution)/shard_map/all_to_all | solution.py:10
  420.5 0.5 reshape.51
  421.1 1.6 copy.26
  422.6 0.0 copy-done.1
  (5 shorter events, 0.0 us)
Async XLA Ops:
  0.6 1.2 copy-start
  7.3 180.0 %slice-start = ((s8[6291456]{0:T(1024)(128)(4,1)}), s8[2097152]{0:T(1024)(128)(4,1)S(1)}, s32[]{:S(2)}) async-start(s8[6291456]{0:T(1024)(128)(4,1)} %bitcast.52), calls=%async_computation.4 | async-start | bytes 4194304
  167.1 4.6 %copy-start.3 = (bf16[64,24,4096]{2,1,0:T(8,128)(2,1)}, bf16[64,24,4096]{2,1,0:T(8,128)(2,1)S(1)}, u32[]{:S(2)}) copy-start(bf16[64,24,4096]{2,1,0:T(8,128)(2,1)S(1)} %all_to_all.21) | copy-start | bytes 37748740
  171.6 15.7 %slice-start.1 = ((s8[6291456]{0:T(1024)(128)(4,1)}), s8[4194304]{0:T(1024)(128)(4,1)S(1)}, s32[]{:S(2)}) async-start(s8[6291456]{0:T(1024)(128)(4,1)} %bitcast.52), calls=%async_computation.5 | async-start | bytes 8388608
  214.7 148.8 %copy-start.4 = (bf16[128,4096]{1,0:T(8,128)(2,1)S(1)}, bf16[128,4096]{1,0:T(8,128)(2,1)}, u32[]{:S(2)}) copy-start(bf16[128,4096]{1,0:T(8,128)(2,1)} %param.13) | copy-start | bytes 3145732
  363.4 4.5 %copy-start.2 = (bf16[64,24,4096]{2,1,0:T(8,128)(2,1)}, bf16[64,24,4096]{2,1,0:T(8,128)(2,1)S(1)}, u32[]{:S(2)}) copy-start(bf16[64,24,4096]{2,1,0:T(8,128)(2,1)S(1)} %all_to_all.22) | copy-start | bytes 37748740
  394.2 1.3 collective-permute-start
  402.0 18.5 %all-to-all-start.3 = ((bf16[64,2,2048]{2,1,0:T(2,128)(2,1)}), bf16[64,2,2048]{2,1,0:T(2,128)(2,1)S(1)}, u32[]{:S(2)}, u32[]{:S(2)}) async-start(bf16[64,2,2048]{2,1,0:T(2,128)(2,1)} %reshape.50), calls=%async_computation.3 | async-start | bytes 1048576 | tf_op jit(solution)/shard_map/all_to_all | solution.py:10
  406.9 15.7 %copy-start.1 = (bf16[128,4096]{1,0:T(8,128)(2,1)S(1)}, bf16[128,4096]{1,0:T(8,128)(2,1)}, u32[]{:S(2)}) copy-start(bf16[128,4096]{1,0:T(8,128)(2,1)} %param.7) | copy-start | bytes 3145732

commit v3 on v2

--- a/solution.py
+++ b/solution.py
@@ -1,20 +1,155 @@
 import jax
 import jax.numpy as jnp
 from jax import lax
+from jax.experimental import pallas as pl
+from jax.experimental.pallas import tpu as pltpu
 from jax.sharding import PartitionSpec as P
 
 GROUP = ("expert", "replica")
+TILE = 256
+SPAN = 1024
+GROUPED = 8
 
 
 def exchange(rows):
     return lax.all_to_all(rows, GROUP, split_axis=0, concat_axis=0, tiled=True)
 
 
+def expert_kernel(rows_ref, gate_hbm, up_hbm, down_hbm, out_ref, gate_mat, up_mat, down_mat, sems):
+    copies = [
+        pltpu.make_async_copy(source, target, sems.at[n])
+        for n, (source, target) in enumerate(
+            ((gate_hbm, gate_mat), (up_hbm, up_mat), (down_hbm, down_mat))
+        )
+    ]
+    first = pl.program_id(0) == 0
+
+    @pl.when(first)
+    def _():
+        for copy in copies:
+            copy.start()
+        copies[0].wait()
+
+    gate_act = jnp.dot(rows_ref[...], gate_mat[...], preferred_element_type=jnp.float32)
+
+    @pl.when(first)
+    def _():
+        copies[1].wait()
+
+    up_act = jnp.dot(rows_ref[...], up_mat[...], preferred_element_type=jnp.float32)
+    hidden = (jax.nn.silu(gate_act) * up_act).astype(jnp.bfloat16)
+
+    @pl.when(first)
+    def _():
+        copies[2].wait()
+
+    width = out_ref.shape[1]
+    for start in range(0, width, SPAN):
+        part = jnp.dot(hidden, down_mat[:, start : start + SPAN], preferred_element_type=jnp.float32)
+        out_ref[:, start : start + SPAN] = part.astype(jnp.bfloat16)
+
+
 def expert_apply(rows, gate_mat, up_mat, down_mat):
-    gate_act = jnp.dot(rows, gate_mat, preferred_element_type=jnp.float32)
-    up_act = jnp.dot(rows, up_mat, preferred_element_type=jnp.float32)
-    hidden = (jax.nn.silu(gate_act) * up_act).astype(jnp.bfloat16)
-    return jnp.dot(hidden, down_mat, preferred_element_type=jnp.float32).astype(jnp.bfloat16)
+    count, width = rows.shape
+    depth = gate_mat.shape[1]
+    whole = pl.BlockSpec(memory_space=pl.ANY)
+    tile = pl.BlockSpec((TILE, width), lambda i: (i, 0))
+    return pl.pallas_call(
+        expert_kernel,
+        out_shape=jax.ShapeDtypeStruct((count, width), jnp.bfloat16),
+        grid=(count // TILE,),
+        in_specs=[tile, whole, whole, whole],
+        out_specs=tile,
+        scratch_shapes=[
+            pltpu.VMEM((width, depth), jnp.bfloat16),
+            pltpu.VMEM((width, depth), jnp.bfloat16),
+            pltpu.VMEM((depth, width), jnp.bfloat16),
+            pltpu.SemaphoreType.DMA((3,)),
+        ],
+        compiler_params=pltpu.CompilerParams(vmem_limit_bytes=60 << 20),
+        name="experts",
+    )(rows, gate_mat, up_mat, down_mat)
+
+
+def column_kernel(rows_ref, scale_ref, out_ref, total):
+    step = pl.program_id(0)
+
+    @pl.when(step == 0)
+    def _():
+        total[...] = jnp.zeros_like(total)
+
+    blocks, slots, width = rows_ref.shape
+    scales = [jnp.broadcast_to(scale_ref[s][:, None], (slots, 128)) for s in range(blocks)]
+    for start in range(0, width, 128):
+        part = total[:, start : start + 128]
+        for s in range(blocks):
+            part = part + rows_ref[s, :, start : start + 128].astype(jnp.float32) * scales[s]
+        total[:, start : start + 128] = part
+
+    @pl.when(step == pl.num_programs(0) - 1)
+    def _():
+        for n in range(width // 128):
+            out_ref[n : n + 1, :] = jnp.sum(total[:, n * 128 : n * 128 + 128], axis=0, keepdims=True)
+
+
+def column_of(rows, scales):
+    sources, slots, width = rows.shape
+    return pl.pallas_call(
+        column_kernel,
+        out_shape=jax.ShapeDtypeStruct((width // 128, 128), jnp.float32),
+        grid=(sources // GROUPED,),
+        in_specs=[
+            pl.BlockSpec((GROUPED, slots, width), lambda i: (i, 0, 0)),
+            pl.BlockSpec((GROUPED, slots), lambda i: (i, 0)),
+        ],
+        out_specs=pl.BlockSpec((width // 128, 128), lambda i: (0, 0)),
+        scratch_shapes=[pltpu.VMEM((slots, width), jnp.float32)],
+        compiler_params=pltpu.CompilerParams(vmem_limit_bytes=60 << 20),
+        name="column",
+    )(rows, scales)
+
+
+def table_kernel(back_ref, cotangent_ref, slot_ref, probs_ref, out_ref, dots):
+    step = pl.program_id(0)
+    blocks, slots, width = back_ref.shape
+    rows = cotangent_ref.shape[0]
+    every = lax.dot_general(
+        back_ref[...].reshape(blocks * slots, width),
+        cotangent_ref[...],
+        (((1,), (1,)), ((), ())),
+        preferred_element_type=jnp.float32,
+    ).reshape(blocks, slots, rows)
+    wanted = lax.broadcasted_iota(jnp.int32, (blocks, slots, rows), 1)
+    pick = slot_ref[...][:, None, :] == wanted
+    dots[pl.ds(pl.multiple_of(step * blocks, blocks), blocks), :] = jnp.sum(
+        jnp.where(pick, every, 0.0), axis=1
+    )
+
+    @pl.when(step == pl.num_programs(0) - 1)
+    def _():
+        probs = probs_ref[...]
+        values = dots[...]
+        out_ref[...] = probs * (values - jnp.sum(probs * values, axis=0, keepdims=True))
+
+
+def table_of(back, cotangent, slot, probs):
+    experts, slots, width = back.shape
+    rows = cotangent.shape[0]
+    return pl.pallas_call(
+        table_kernel,
+        out_shape=jax.ShapeDtypeStruct((experts, rows), jnp.float32),
+        grid=(experts // GROUPED,),
+        in_specs=[
+            pl.BlockSpec((GROUPED, slots, width), lambda i: (i, 0, 0)),
+            pl.BlockSpec((rows, width), lambda i: (0, 0)),
+            pl.BlockSpec((GROUPED, rows), lambda i: (i, 0)),
+            pl.BlockSpec((experts, rows), lambda i: (0, 0)),
+        ],
+        out_specs=pl.BlockSpec((experts, rows), lambda i: (0, 0)),
+        scratch_shapes=[pltpu.VMEM((experts, rows), jnp.float32)],
+        compiler_params=pltpu.CompilerParams(vmem_limit_bytes=60 << 20),
+        name="table",
+    )(back, cotangent, slot, probs)
 
 
 def local(tokens, expert_ids, router_weight, gate_weight, up_weight, down_weight, cotangent):
@@ -46,20 +181,17 @@
     back = exchange(out.reshape(experts, capacity, model_width)).reshape(-1, model_width)
 
     pick = slot[:, None, :] == wanted[None, :, None]
-    every = lax.dot_general(
-        back, cotangent, (((1,), (1,)), ((), ())), preferred_element_type=jnp.float32
-    ).reshape(experts, capacity, tok_rows)
-    dots = jnp.sum(jnp.where(pick, every, 0.0), axis=1)
-    table = probs * (dots - jnp.sum(probs * dots, axis=0, keepdims=True))
+    table = table_of(back.reshape(experts, capacity, model_width), cotangent, slot, probs)
     slot_grad = jnp.sum(jnp.where(pick, table[:, None, :], 0.0), axis=2)
     theirs = exchange(slot_grad[:, None, :])
     share = jnp.where(pick, probs[:, None, :], 0.0).astype(jnp.bfloat16).reshape(-1, tok_rows)
     mixed = lax.dot_general(
         share, back, (((0,), (0,)), ((), ())), preferred_element_type=jnp.float32
     ).astype(jnp.bfloat16)
-    row = jnp.sum(rows.astype(jnp.float32) * theirs.reshape(-1, 1), axis=0, keepdims=True)
-    row = row + lax.ppermute(row, "dp", [(0, 1), (1, 0)])
-    columns = exchange(jnp.broadcast_to(row.astype(jnp.bfloat16), (experts, model_width)))
+    column = column_of(rows.reshape(experts, capacity, model_width), theirs.reshape(experts, capacity))
+    column = column + lax.ppermute(column, "dp", [(0, 1), (1, 0)])
+    columns = exchange(jnp.broadcast_to(column.astype(jnp.bfloat16), (experts,) + column.shape))
+    columns = columns.reshape(experts, model_width)
     return (mixed, columns.astype(jnp.float32).T)
 
 

time: 423 us -> 430 us (1.017)
  Pallas kernels: 0 us -> 63.3 us
  matrix products: 59.6 us -> 24.9 us
  other arithmetic: 13.2 us -> 3.56 us
  local copies, waits for them, and re-layouts: 10.4 us -> 2.38 us
  waiting for transfers between devices: 7.3 us -> 1.39 us
    pallas_call x0 -> x3, Pallas kernels: none -> 63.3 us  [the longest x1 44.7 us: expert_apply(): pl.pallas_call(expert_kernel, out_shape=jax.ShapeDtypeStruct((count, widt...]
    dot_general x4 -> x0, matrix products: 46.9 us -> none  [the longest x1 15.7 us: expert_apply(): up_act = jnp.dot(rows, up_mat, preferred_element_type=jnp.float32)]
    dot_general x1, matrix products: 7.47 us -> 19.6 us  [local(): lax.dot_general(share, back, (((0,), (0,)), ((), ())), preferred_element_...]
    reduce_sum x2 -> x0, other arithmetic: 7.98 us -> none  [the longest x1 7.96 us: local(): jnp.sum(rows.astype(jnp.float32) * theirs.reshape(-1, 1), axis=0, keepdim...]
    unnamed x18 -> x11, local copies, waits for them, and re-layouts: 8.68 us -> 1.35 us
    all_to_all x1, waiting for transfers between devices: 6.13 us -> 0.01 us  [exchange(): return lax.all_to_all(rows, GROUP, split_axis=0, concat_axis=0, tiled=True)]
  transfers between devices with their start and end apart: 2 -> 2, of which waited for: 2 -> 1; matrix products, arithmetic and copies ran while one was open for 2% -> 5% of each run, Pallas kernels for 0% -> 0%
where the time goes in v3:
time: 430 us; the launch traced here: 429 us
  blocking collectives  327 us (76%)
  Pallas kernels  63.3 us (15%)
  matrix products  24.9 us (6%)
  starting transfers between devices  5.2 us (1%)
    all_to_all x3, blocking collectives, exchange(): return lax.all_to_all(rows, GROUP, split_axis=0, concat_axis=0, tiled=True)  327 us
    pallas_call x1, Pallas kernels, expert_apply(): pl.pallas_call(expert_kernel, out_shape=jax.ShapeDtypeStruct((count, widt...  44.7 us
    dot_general x1, matrix products, local(): lax.dot_general(share, back, (((0,), (0,)), ((), ())), preferred_element_...  19.6 us
    pallas_call x1, Pallas kernels, table_of(): pl.pallas_call(table_kernel, out_shape=jax.ShapeDtypeStruct((experts, row...  9.93 us
    pallas_call x1, Pallas kernels, column_of(): pl.pallas_call(column_kernel, out_shape=jax.ShapeDtypeStruct((width // 12...  8.65 us
  transfers between devices with their start and end apart: 2, of which 1 were waited for; matrix products, arithmetic and copies ran while one was open for 5% of the time, Pallas kernels for 0%

profile of v3, /device:TPU:0, one launch (start us, length us, event | category | flops | bytes accessed | tf_op | source)
XLA Modules:
  0.0 428.6 jit_solution(13255092346159074983)
XLA Ops:
  0.6 0.0 copy-start
  0.6 0.8 fusion.13
  1.5 0.1 fusion.9.slot_ref
  1.6 0.0 copy-start.2
  1.6 0.1 eq.52
  1.7 0.2 copy-done
  1.9 1.5 fusion.15
  3.4 0.3 bitcast_compare_fusion
  3.7 3.6 convolution_convert_fusion
  7.3 0.6 broadcast_divide_fusion.probs_ref
  7.9 159.7 %all_to_all.20.rows_ref = bf16[64,24,4096]{2,1,0:T(8,128)(2,1)} all-to-all(bf16[64,24,4096]{2,1,0:T(8,128)(2,1)S(1)} %bitcast.29), channel_id=1, replica_groups=mesh['dp'=2,'expert'=32,'replica'=2] {'expert','replica'}, dimensions={0} | all-to-all | bytes 25165824 | tf_op jit(solution)/shard_map/all_to_all | solution.py:15
  167.7 0.0 copy-done.2
  167.7 44.7 %experts.1 = bf16[1536,4096]{1,0:T(8,128)(2,1)} custom-call(bf16[1536,4096]{1,0:T(8,128)(2,1)} %bitcast.28, bf16[4096,768]{1,0:T(8,128)(2,1)} %bitcast.31, bf16[4096,768]{1,0:T(8,128)(2,1)} %bitcast.32, bf16[768,4096]{1,0:T(8,128)(2,1)} %bitcast.33), custom_call_target="tpu_custom_call" | custom-call | tf_op jit(solution)/shard_map/experts/pallas_call | solution.py:57
  212.4 151.1 %all_to_all.21.back_ref = bf16[64,24,4096]{2,1,0:T(8,128)(2,1)} all-to-all(bf16[64,24,4096]{2,1,0:T(8,128)(2,1)} %bitcast.30), channel_id=1, replica_groups=mesh['dp'=2,'expert'=32,'replica'=2] {'expert','replica'}, dimensions={0} | all-to-all | bytes 25165824 | tf_op jit(solution)/shard_map/all_to_all | solution.py:15
  363.5 0.0 copy-start.3
  363.5 0.0 copy-start.4
  363.5 9.9 %table.1 = f32[64,128]{1,0:T(8,128)} custom-call(bf16[64,24,4096]{2,1,0:T(8,128)(2,1)} %all_to_all.21.back_ref, bf16[128,4096]{1,0:T(8,128)(2,1)} %cotangent_ref.1, s32[64,128]{1,0:T(8,128)} %copy-done.2, f32[64,128]{1,0:T(8,128)} %broadcast_divide_fusion.probs_ref), custom_call_target="tpu_custom_call" | custom-call | tf_op jit(solution)/shard_map/table/pallas_call | solution.py:138
  373.4 0.0 copy-done.3
  373.4 1.0 select_reduce_fusion
  374.4 0.1 copy.14
  374.5 16.4 %all_to_all.22 = f32[64,1,24]{2,1,0:T(1,128)} all-to-all(f32[64,1,24]{2,1,0:T(1,128)S(1)} %copy.14), channel_id=1, replica_groups=mesh['dp'=2,'expert'=32,'replica'=2] {'expert','replica'}, dimensions={0} | all-to-all | bytes 12288 | tf_op jit(solution)/shard_map/all_to_all | solution.py:15
  390.9 8.6 %column.1 = f32[32,128]{1,0:T(8,128)} custom-call(bf16[64,24,4096]{2,1,0:T(8,128)(2,1)} %all_to_all.20.rows_ref, f32[64,24]{1,0:T(8,128)} %bitcast.36), custom_call_target="tpu_custom_call" | custom-call | tf_op jit(solution)/shard_map/column/pallas_call | solution.py:97
  399.6 0.0 collective-permute-start
  399.6 1.4 collective-permute-done
  400.9 0.0 copy-start.1
  400.9 0.8 add_convert_fusion
  401.8 0.9 broadcast_in_dim.49
  402.6 5.2 %all-to-all-start.3 = ((bf16[64,32,128]{2,1,0:T(8,128)(2,1)}), bf16[64,32,128]{2,1,0:T(8,128)(2,1)S(1)}, u32[]{:S(2)}, u32[]{:S(2)}) async-start(bf16[64,32,128]{2,1,0:T(8,128)(2,1)} %broadcast_in_dim.49), calls=%async_computation.3 | async-start | bytes 1048576 | tf_op jit(solution)/shard_map/all_to_all | solution.py:15
  407.8 0.0 copy-done.4
  407.8 19.6 %fusion.5 = bf16[128,4096]{1,0:T(8,128)(2,1)} fusion(bf16[64,24,4096]{2,1,0:T(8,128)(2,1)} %all_to_all.21.back_ref, f32[64,128]{1,0:T(8,128)S(1)} %copy-done.4, s32[64,128]{1,0:T(8,128)S(1)} %copy-done.3), kind=kOutput, calls=%fused_computation.4 | convolution fusion | flops 1611530240 | bytes 13697024 | tf_op jit(solution)/shard_map/dot_general | solution.py:188
  427.5 0.0 all-to-all-done.3
  427.5 1.1 copy.23
  428.6 0.0 copy-done.1
  (1 shorter events, 0.0 us)
Async XLA Ops:
  0.6 1.2 copy-start
  1.6 166.1 %copy-start.2 = (s32[64,128]{1,0:T(8,128)}, s32[64,128]{1,0:T(8,128)S(1)}, u32[]{:S(2)}) copy-start(s32[64,128]{1,0:T(8,128)S(1)} %fusion.9.slot_ref) | copy-start | bytes 98308
  363.5 9.9 %copy-start.3 = (s32[64,128]{1,0:T(8,128)S(1)}, s32[64,128]{1,0:T(8,128)}, u32[]{:S(2)}) copy-start(s32[64,128]{1,0:T(8,128)} %copy-done.2) | copy-start | bytes 98308
  363.5 44.4 %copy-start.4 = (f32[64,128]{1,0:T(8,128)S(1)}, f32[64,128]{1,0:T(8,128)}, u32[]{:S(2)}) copy-start(f32[64,128]{1,0:T(8,128)} %broadcast_divide_fusion.probs_ref) | copy-start | bytes 98308
  399.6 1.4 collective-permute-start
  400.9 27.7 %copy-start.1 = (bf16[128,4096]{1,0:T(8,128)(2,1)S(1)}, bf16[128,4096]{1,0:T(8,128)(2,1)}, u32[]{:S(2)}) copy-start(bf16[128,4096]{1,0:T(8,128)(2,1)} %param.7) | copy-start | bytes 3145732
  402.6 24.8 %all-to-all-start.3 = ((bf16[64,32,128]{2,1,0:T(8,128)(2,1)}), bf16[64,32,128]{2,1,0:T(8,128)(2,1)S(1)}, u32[]{:S(2)}, u32[]{:S(2)}) async-start(bf16[64,32,128]{2,1,0:T(8,128)(2,1)} %broadcast_in_dim.49), calls=%async_computation.3 | async-start | bytes 1048576 | tf_op jit(solution)/shard_map/all_to_all | solution.py:15

commit v4 on v3

--- a/solution.py
+++ b/solution.py
@@ -6,9 +6,11 @@
 from jax.sharding import PartitionSpec as P
 
 GROUP = ("expert", "replica")
-TILE = 256
-SPAN = 1024
-GROUPED = 8
+TILE = 384
+SPAN = 512
+GROUPED = 32
+PIECES = 16
+SPANM = 2048
 
 
 def exchange(rows):
@@ -71,39 +73,56 @@
     )(rows, gate_mat, up_mat, down_mat)
 
 
-def column_kernel(rows_ref, scale_ref, out_ref, total):
-    step = pl.program_id(0)
-
-    @pl.when(step == 0)
-    def _():
-        total[...] = jnp.zeros_like(total)
-
-    blocks, slots, width = rows_ref.shape
-    scales = [jnp.broadcast_to(scale_ref[s][:, None], (slots, 128)) for s in range(blocks)]
-    for start in range(0, width, 128):
-        part = total[:, start : start + 128]
-        for s in range(blocks):
-            part = part + rows_ref[s, :, start : start + 128].astype(jnp.float32) * scales[s]
-        total[:, start : start + 128] = part
-
-    @pl.when(step == pl.num_programs(0) - 1)
-    def _():
-        for n in range(width // 128):
-            out_ref[n : n + 1, :] = jnp.sum(total[:, n * 128 : n * 128 + 128], axis=0, keepdims=True)
+def fetch(source, target, sems):
+    count = source.shape[0] // PIECES
+    copies = []
+    for n in range(PIECES):
+        cut = pl.ds(n * count, count)
+        copies.append(pltpu.make_async_copy(source.at[cut], target.at[cut], sems.at[n]))
+    for copy in copies:
+        copy.start()
+    return count, copies
+
+
+def column_kernel(rows_hbm, scale_ref, out_ref, rows, total, sems):
+    count, copies = fetch(rows_hbm, rows, sems)
+    _, slots, width = rows.shape
+    for n, copy in enumerate(copies):
+        scales = [
+            jnp.broadcast_to(scale_ref[s][:, None], (slots, 128))
+            for s in range(n * count, n * count + count)
+        ]
+        copy.wait()
+        for start in range(0, width, 128):
+            lanes = slice(start, start + 128)
+            part = [
+                rows[n * count + s, :, lanes].astype(jnp.float32) * scales[s] for s in range(count)
+            ]
+            while len(part) > 1:
+                part = [a + b for a, b in zip(part[::2], part[1::2])]
+            if n == 0:
+                total[:, lanes] = part[0]
+            elif n < PIECES - 1:
+                total[:, lanes] += part[0]
+            else:
+                out_ref[start // 128 : start // 128 + 1, :] = jnp.sum(
+                    total[:, lanes] + part[0], axis=0, keepdims=True
+                )
 
 
 def column_of(rows, scales):
-    sources, slots, width = rows.shape
+    _, slots, width = rows.shape
+    near = pl.BlockSpec(memory_space=pltpu.VMEM)
     return pl.pallas_call(
         column_kernel,
         out_shape=jax.ShapeDtypeStruct((width // 128, 128), jnp.float32),
-        grid=(sources // GROUPED,),
-        in_specs=[
-            pl.BlockSpec((GROUPED, slots, width), lambda i: (i, 0, 0)),
-            pl.BlockSpec((GROUPED, slots), lambda i: (i, 0)),
-        ],
-        out_specs=pl.BlockSpec((width // 128, 128), lambda i: (0, 0)),
-        scratch_shapes=[pltpu.VMEM((slots, width), jnp.float32)],
+        in_specs=[pl.BlockSpec(memory_space=pl.ANY), near],
+        out_specs=near,
+        scratch_shapes=[
+            pltpu.VMEM(rows.shape, jnp.bfloat16),
+            pltpu.VMEM((slots, width), jnp.float32),
+            pltpu.SemaphoreType.DMA((PIECES,)),
+        ],
         compiler_params=pltpu.CompilerParams(vmem_limit_bytes=60 << 20),
         name="column",
     )(rows, scales)
@@ -152,6 +171,41 @@
     )(back, cotangent, slot, probs)
 
 
+def mixed_kernel(back_ref, slot_ref, probs_ref, out_ref, share):
+    blocks, slots, width = back_ref.shape
+    rows = out_ref.shape[0]
+
+    @pl.when(pl.program_id(0) == 0)
+    def _():
+        wanted = lax.broadcasted_iota(jnp.int32, (blocks, slots, rows), 1)
+        pick = slot_ref[...][:, None, :] == wanted
+        chosen = jnp.where(pick, probs_ref[...][:, None, :], 0.0)
+        share[...] = chosen.reshape(blocks * slots, rows).T.astype(jnp.bfloat16)
+
+    out_ref[...] = jnp.dot(
+        share[...], back_ref[...].reshape(blocks * slots, width), preferred_element_type=jnp.float32
+    ).astype(jnp.bfloat16)
+
+
+def mixed_of(back, slot, probs):
+    experts, slots, width = back.shape
+    rows = slot.shape[1]
+    return pl.pallas_call(
+        mixed_kernel,
+        out_shape=jax.ShapeDtypeStruct((rows, width), jnp.bfloat16),
+        grid=(width // SPANM,),
+        in_specs=[
+            pl.BlockSpec((experts, slots, SPANM), lambda i: (0, 0, i)),
+            pl.BlockSpec((experts, rows), lambda i: (0, 0)),
+            pl.BlockSpec((experts, rows), lambda i: (0, 0)),
+        ],
+        out_specs=pl.BlockSpec((rows, SPANM), lambda i: (0, i)),
+        scratch_shapes=[pltpu.VMEM((rows, experts * slots), jnp.bfloat16)],
+        compiler_params=pltpu.CompilerParams(vmem_limit_bytes=60 << 20),
+        name="mixed",
+    )(back, slot, probs)
+
+
 def local(tokens, expert_ids, router_weight, gate_weight, up_weight, down_weight, cotangent):
     tok_rows, model_width = tokens.shape
     top_count = expert_ids.shape[1]
@@ -184,10 +238,7 @@
     table = table_of(back.reshape(experts, capacity, model_width), cotangent, slot, probs)
     slot_grad = jnp.sum(jnp.where(pick, table[:, None, :], 0.0), axis=2)
     theirs = exchange(slot_grad[:, None, :])
-    share = jnp.where(pick, probs[:, None, :], 0.0).astype(jnp.bfloat16).reshape(-1, tok_rows)
-    mixed = lax.dot_general(
-        share, back, (((0,), (0,)), ((), ())), preferred_element_type=jnp.float32
-    ).astype(jnp.bfloat16)
+    mixed = mixed_of(back.reshape(experts, capacity, model_width), slot, probs)
     column = column_of(rows.reshape(experts, capacity, model_width), theirs.reshape(experts, capacity))
     column = column + lax.ppermute(column, "dp", [(0, 1), (1, 0)])
     columns = exchange(jnp.broadcast_to(column.astype(jnp.bfloat16), (experts,) + column.shape))

time: 430 us -> 419 us (0.974)
  matrix products: 24.9 us -> 5.27 us
  waiting for transfers between devices: 1.39 us -> 8.53 us
    dot_general x1 -> x0, matrix products: 19.6 us -> none  [local(): lax.dot_general(share, back, (((0,), (0,)), ((), ())), preferred_element_...]
    all_to_all x1, waiting for transfers between devices: 0.01 us -> 7.15 us  [exchange(): return lax.all_to_all(rows, GROUP, split_axis=0, concat_axis=0, tiled=True)]
    pallas_call x0 -> x1, Pallas kernels: none -> 6.45 us  [mixed_of(): pl.pallas_call(mixed_kernel, out_shape=jax.ShapeDtypeStruct((rows, width)...]
  transfers between devices with their start and end apart: 2 -> 2, of which waited for: 1 -> 2; matrix products, arithmetic and copies ran while one was open for 5% -> 0% of each run, Pallas kernels for 0% -> 2%
where the time goes in v4:
time: 419 us
  blocking collectives  328 us (78%)
  Pallas kernels  65.7 us (16%)
  waiting for transfers between devices  8.53 us (2%)
  matrix products  5.27 us (1%)
  starting transfers between devices  5.1 us (1%)
    all_to_all x3, blocking collectives, exchange(): return lax.all_to_all(rows, GROUP, split_axis=0, concat_axis=0, tiled=True)  328 us
    pallas_call x1, Pallas kernels, expert_apply(): pl.pallas_call(expert_kernel, out_shape=jax.ShapeDtypeStruct((count, widt...  44.3 us
    pallas_call x1, Pallas kernels, table_of(): pl.pallas_call(table_kernel, out_shape=jax.ShapeDtypeStruct((experts, row...  8.59 us
  transfers between devices with their start and end apart: 2, of which 2 were waited for; matrix products, arithmetic and copies ran while one was open for 0% of the time, Pallas kernels for 2%

profile of v4, /device:TPU:0, one launch (start us, length us, event | category | flops | bytes accessed | tf_op | source)
XLA Modules:
  0.0 418.6 jit_solution(10254316572173929278)
XLA Ops:
  0.6 0.0 copy-start
  0.6 0.8 fusion.2
  1.5 0.1 fusion.1.slot_ref
  1.6 0.0 copy-start.2
  1.6 0.1 eq.52
  1.7 0.2 copy-done
  1.9 1.5 fusion.3
  3.4 0.3 bitcast_compare_fusion
  3.7 3.6 convolution_convert_fusion
  7.3 0.6 broadcast_divide_fusion.probs_ref
  7.9 159.7 %all_to_all.20.rows_hbm = bf16[64,24,4096]{2,1,0:T(8,128)(2,1)} all-to-all(bf16[64,24,4096]{2,1,0:T(8,128)(2,1)S(1)} %bitcast.27), channel_id=1, replica_groups=mesh['dp'=2,'expert'=32,'replica'=2] {'expert','replica'}, dimensions={0} | all-to-all | bytes 25165824 | tf_op jit(solution)/shard_map/all_to_all | solution.py:17
  167.7 0.0 copy-done.2
  167.7 44.3 %experts.1 = bf16[1536,4096]{1,0:T(8,128)(2,1)} custom-call(bf16[1536,4096]{1,0:T(8,128)(2,1)} %bitcast.26, bf16[4096,768]{1,0:T(8,128)(2,1)} %bitcast.29, bf16[4096,768]{1,0:T(8,128)(2,1)} %bitcast.30, bf16[768,4096]{1,0:T(8,128)(2,1)} %bitcast.31), custom_call_target="tpu_custom_call" | custom-call | tf_op jit(solution)/shard_map/experts/pallas_call | solution.py:59
  212.0 151.8 %all_to_all.21.back_ref = bf16[64,24,4096]{2,1,0:T(8,128)(2,1)} all-to-all(bf16[64,24,4096]{2,1,0:T(8,128)(2,1)} %bitcast.28), channel_id=1, replica_groups=mesh['dp'=2,'expert'=32,'replica'=2] {'expert','replica'}, dimensions={0} | all-to-all | bytes 25165824 | tf_op jit(solution)/shard_map/all_to_all | solution.py:17
  363.8 0.0 copy-start.3
  363.8 8.6 %table.1 = f32[64,128]{1,0:T(8,128)} custom-call(bf16[64,24,4096]{2,1,0:T(8,128)(2,1)} %all_to_all.21.back_ref, bf16[128,4096]{1,0:T(8,128)(2,1)} %cotangent_ref.1, s32[64,128]{1,0:T(8,128)} %copy-done.2, f32[64,128]{1,0:T(8,128)} %broadcast_divide_fusion.probs_ref), custom_call_target="tpu_custom_call" | custom-call | tf_op jit(solution)/shard_map/table/pallas_call | solution.py:157
  372.4 0.0 copy-done.3
  372.4 1.0 select_reduce_fusion
  373.5 15.9 %all_to_all.22 = f32[64,1,24]{2,1,0:T(1,128)} all-to-all(f32[64,1,24]{2,1,0:T(1,128)S(1)} %bitcast.35), channel_id=1, replica_groups=mesh['dp'=2,'expert'=32,'replica'=2] {'expert','replica'}, dimensions={0} | all-to-all | bytes 12288 | tf_op jit(solution)/shard_map/all_to_all | solution.py:17
  389.4 0.0 copy-start.1
  389.4 6.4 %column.1 = f32[32,128]{1,0:T(8,128)} custom-call(bf16[64,24,4096]{2,1,0:T(8,128)(2,1)} %all_to_all.20.rows_hbm, f32[64,24]{1,0:T(8,128)} %bitcast.34), custom_call_target="tpu_custom_call" | custom-call | tf_op jit(solution)/shard_map/column/pallas_call | solution.py:116
  395.8 0.1 collective-permute-start
  395.9 1.4 collective-permute-done
  397.3 0.7 add_convert_fusion
  398.0 0.9 broadcast_in_dim.41
  398.9 5.0 %all-to-all-start.3 = ((bf16[64,32,128]{2,1,0:T(8,128)(2,1)}), bf16[64,32,128]{2,1,0:T(8,128)(2,1)S(1)}, u32[]{:S(2)}, u32[]{:S(2)}) async-start(bf16[64,32,128]{2,1,0:T(8,128)(2,1)} %broadcast_in_dim.41), calls=%async_computation.3 | async-start | bytes 1048576 | tf_op jit(solution)/shard_map/all_to_all | solution.py:17
  403.9 6.5 %mixed.1 = bf16[128,4096]{1,0:T(8,128)(2,1)} custom-call(bf16[64,24,4096]{2,1,0:T(8,128)(2,1)} %all_to_all.21.back_ref, s32[64,128]{1,0:T(8,128)} %copy-done.2, f32[64,128]{1,0:T(8,128)} %broadcast_divide_fusion.probs_ref), custom_call_target="tpu_custom_call" | custom-call | tf_op jit(solution)/shard_map/mixed/pallas_call | solution.py:193
  410.3 7.1 %all-to-all-done.3 = bf16[64,32,128]{2,1,0:T(8,128)(2,1)S(1)} async-done(((bf16[64,32,128]{2,1,0:T(8,128)(2,1)}), bf16[64,32,128]{2,1,0:T(8,128)(2,1)S(1)}, u32[]{:S(2)}, u32[]{:S(2)}) %all-to-all-start.3) | async-done | bytes 524320 | tf_op jit(solution)/shard_map/all_to_all | solution.py:17
  417.5 1.1 copy.12
  418.6 0.0 copy-done.1
  (1 shorter events, 0.0 us)
Async XLA Ops:
  0.6 1.2 copy-start
  1.6 166.1 %copy-start.2 = (s32[64,128]{1,0:T(8,128)}, s32[64,128]{1,0:T(8,128)S(1)}, u32[]{:S(2)}) copy-start(s32[64,128]{1,0:T(8,128)S(1)} %fusion.1.slot_ref) | copy-start | bytes 98308
  363.8 8.6 %copy-start.3 = (s32[64,128]{1,0:T(8,128)S(1)}, s32[64,128]{1,0:T(8,128)}, u32[]{:S(2)}) copy-start(s32[64,128]{1,0:T(8,128)} %copy-done.2) | copy-start | bytes 98308
  389.4 29.2 %copy-start.1 = (bf16[128,4096]{1,0:T(8,128)(2,1)S(1)}, bf16[128,4096]{1,0:T(8,128)(2,1)}, u32[]{:S(2)}) copy-start(bf16[128,4096]{1,0:T(8,128)(2,1)} %param.7) | copy-start | bytes 3145732
  395.8 1.5 collective-permute-start
  398.9 18.6 %all-to-all-start.3 = ((bf16[64,32,128]{2,1,0:T(8,128)(2,1)}), bf16[64,32,128]{2,1,0:T(8,128)(2,1)S(1)}, u32[]{:S(2)}, u32[]{:S(2)}) async-start(bf16[64,32,128]{2,1,0:T(8,128)(2,1)} %broadcast_in_dim.41), calls=%async_computation.3 | async-start | bytes 1048576 | tf_op jit(solution)/shard_map/all_to_all | solution.py:17

commit v5 on v4

--- a/solution.py
+++ b/solution.py
@@ -6,7 +6,8 @@
 from jax.sharding import PartitionSpec as P
 
 GROUP = ("expert", "replica")
-TILE = 384
+EARLY = 16
+BLOCKS = 32
 SPAN = 512
 GROUPED = 32
 PIECES = 16
@@ -17,7 +18,8 @@
     return lax.all_to_all(rows, GROUP, split_axis=0, concat_axis=0, tiled=True)
 
 
-def expert_kernel(rows_ref, gate_hbm, up_hbm, down_hbm, out_ref, gate_mat, up_mat, down_mat, sems):
+def expert_kernel(rows_ref, gate_hbm, up_hbm, down_hbm, *rest):
+    out_ref, gate_mat, up_mat, down_mat, sems = rest[-5:]
     copies = [
         pltpu.make_async_copy(source, target, sems.at[n])
         for n, (source, target) in enumerate(
@@ -32,100 +34,123 @@
             copy.start()
         copies[0].wait()
 
-    gate_act = jnp.dot(rows_ref[...], gate_mat[...], preferred_element_type=jnp.float32)
+    blocks, slots, width = rows_ref.shape
+    flat = (blocks * slots, width)
+    gate_act = jnp.dot(
+        rows_ref[...].reshape(flat), gate_mat[...], preferred_element_type=jnp.float32
+    )
 
     @pl.when(first)
     def _():
         copies[1].wait()
 
-    up_act = jnp.dot(rows_ref[...], up_mat[...], preferred_element_type=jnp.float32)
+    up_act = jnp.dot(rows_ref[...].reshape(flat), up_mat[...], preferred_element_type=jnp.float32)
     hidden = (jax.nn.silu(gate_act) * up_act).astype(jnp.bfloat16)
 
     @pl.when(first)
     def _():
         copies[2].wait()
 
-    width = out_ref.shape[1]
     for start in range(0, width, SPAN):
         part = jnp.dot(hidden, down_mat[:, start : start + SPAN], preferred_element_type=jnp.float32)
-        out_ref[:, start : start + SPAN] = part.astype(jnp.bfloat16)
-
-
-def expert_apply(rows, gate_mat, up_mat, down_mat):
-    count, width = rows.shape
+        out_ref[:, :, start : start + SPAN] = part.astype(jnp.bfloat16).reshape(blocks, slots, SPAN)
+
+
+def expert_apply(rows, gate_mat, up_mat, down_mat, capacity, place, into=None):
+    sources, slots, width = rows.shape
     depth = gate_mat.shape[1]
     whole = pl.BlockSpec(memory_space=pl.ANY)
-    tile = pl.BlockSpec((TILE, width), lambda i: (i, 0))
+    held = [] if into is None else [into]
     return pl.pallas_call(
         expert_kernel,
-        out_shape=jax.ShapeDtypeStruct((count, width), jnp.bfloat16),
-        grid=(count // TILE,),
-        in_specs=[tile, whole, whole, whole],
-        out_specs=tile,
+        out_shape=jax.ShapeDtypeStruct((sources, capacity, width), jnp.bfloat16),
+        grid=(sources // BLOCKS,),
+        in_specs=[pl.BlockSpec((BLOCKS, slots, width), lambda i: (i, 0, 0)), whole, whole, whole]
+        + [whole] * len(held),
+        out_specs=pl.BlockSpec((BLOCKS, slots, width), lambda i: (i, place, 0)),
         scratch_shapes=[
             pltpu.VMEM((width, depth), jnp.bfloat16),
             pltpu.VMEM((width, depth), jnp.bfloat16),
             pltpu.VMEM((depth, width), jnp.bfloat16),
             pltpu.SemaphoreType.DMA((3,)),
         ],
-        compiler_params=pltpu.CompilerParams(vmem_limit_bytes=60 << 20),
+        input_output_aliases={4: 0} if held else {},
+        compiler_params=pltpu.CompilerParams(vmem_limit_bytes=60 << 20),
+        cost_estimate=pl.CostEstimate(
+            flops=6 * sources * slots * width * depth,
+            bytes_accessed=2 * (2 * sources * slots * width + 3 * width * depth),
+            transcendentals=sources * slots * depth,
+        ),
         name="experts",
-    )(rows, gate_mat, up_mat, down_mat)
-
-
-def fetch(source, target, sems):
-    count = source.shape[0] // PIECES
+    )(rows, gate_mat, up_mat, down_mat, *held)
+
+
+def column_kernel(early_hbm, late_hbm, scale_ref, out_ref, early, late, total, sems):
+    count = early.shape[0] // PIECES
+    parts = ((early_hbm, early), (late_hbm, late))
     copies = []
     for n in range(PIECES):
         cut = pl.ds(n * count, count)
-        copies.append(pltpu.make_async_copy(source.at[cut], target.at[cut], sems.at[n]))
-    for copy in copies:
-        copy.start()
-    return count, copies
-
-
-def column_kernel(rows_hbm, scale_ref, out_ref, rows, total, sems):
-    count, copies = fetch(rows_hbm, rows, sems)
-    _, slots, width = rows.shape
-    for n, copy in enumerate(copies):
+        copies.append(
+            [
+                pltpu.make_async_copy(source.at[cut], target.at[cut], sems.at[k, n])
+                for k, (source, target) in enumerate(parts)
+            ]
+        )
+    for pair in copies:
+        for copy in pair:
+            copy.start()
+    first = early.shape[1]
+    slots = first + late.shape[1]
+    width = early.shape[2]
+    for n, pair in enumerate(copies):
         scales = [
             jnp.broadcast_to(scale_ref[s][:, None], (slots, 128))
             for s in range(n * count, n * count + count)
         ]
-        copy.wait()
+        for copy in pair:
+            copy.wait()
         for start in range(0, width, 128):
             lanes = slice(start, start + 128)
-            part = [
-                rows[n * count + s, :, lanes].astype(jnp.float32) * scales[s] for s in range(count)
-            ]
+            part = []
+            for s in range(count):
+                row = n * count + s
+                part.append(early[row, :, lanes].astype(jnp.float32) * scales[s][:first])
             while len(part) > 1:
                 part = [a + b for a, b in zip(part[::2], part[1::2])]
+            part = [part[0][k : k + 8] for k in range(0, first, 8)]
+            for s in range(count):
+                row = n * count + s
+                part.append(late[row, :, lanes].astype(jnp.float32) * scales[s][first:])
+            part = sum(part[1:], part[0])
             if n == 0:
-                total[:, lanes] = part[0]
+                total[:, lanes] = part
             elif n < PIECES - 1:
-                total[:, lanes] += part[0]
+                total[:, lanes] += part
             else:
                 out_ref[start // 128 : start // 128 + 1, :] = jnp.sum(
-                    total[:, lanes] + part[0], axis=0, keepdims=True
+                    total[:, lanes] + part, axis=0, keepdims=True
                 )
 
 
-def column_of(rows, scales):
-    _, slots, width = rows.shape
+def column_of(early, late, scales):
+    width = early.shape[2]
     near = pl.BlockSpec(memory_space=pltpu.VMEM)
+    whole = pl.BlockSpec(memory_space=pl.ANY)
     return pl.pallas_call(
         column_kernel,
         out_shape=jax.ShapeDtypeStruct((width // 128, 128), jnp.float32),
-        in_specs=[pl.BlockSpec(memory_space=pl.ANY), near],
+        in_specs=[whole, whole, near],
         out_specs=near,
         scratch_shapes=[
-            pltpu.VMEM(rows.shape, jnp.bfloat16),
-            pltpu.VMEM((slots, width), jnp.float32),
-            pltpu.SemaphoreType.DMA((PIECES,)),
+            pltpu.VMEM(early.shape, jnp.bfloat16),
+            pltpu.VMEM(late.shape, jnp.bfloat16),
+            pltpu.VMEM((late.shape[1], width), jnp.float32),
+            pltpu.SemaphoreType.DMA((2, PIECES)),
         ],
         compiler_params=pltpu.CompilerParams(vmem_limit_bytes=60 << 20),
         name="column",
-    )(rows, scales)
+    )(early, late, scales)
 
 
 def table_kernel(back_ref, cotangent_ref, slot_ref, probs_ref, out_ref, dots):
@@ -219,27 +244,32 @@
     slot = jnp.where(member, before.astype(jnp.int32), -1)
 
     wanted = jnp.arange(capacity, dtype=jnp.int32)
-    pick = slot[:, None, :] == wanted[None, :, None]
     logits = lax.dot_general(
         router_weight, tokens, (((0,), (1,)), ((), ())), preferred_element_type=jnp.float32
     )
     raised = jnp.where(member, jnp.exp(logits), 0.0)
     probs = raised / jnp.sum(raised, axis=0, keepdims=True)
-    box = jnp.dot(
-        pick.reshape(-1, tok_rows).astype(jnp.bfloat16), tokens, preferred_element_type=jnp.float32
-    ).astype(jnp.bfloat16)
-    box, probs, slot = lax.optimization_barrier((box, probs, slot))
-
-    rows = exchange(box.reshape(experts, capacity, model_width)).reshape(-1, model_width)
-    out = expert_apply(rows, gate_weight[0], up_weight[0], down_weight[0])
-    back = exchange(out.reshape(experts, capacity, model_width)).reshape(-1, model_width)
+    boxes = []
+    for numbers in (wanted[:EARLY], wanted[EARLY:]):
+        pick = (slot[:, None, :] == numbers[None, :, None]).reshape(-1, tok_rows)
+        box = jnp.dot(pick.astype(jnp.bfloat16), tokens, preferred_element_type=jnp.float32)
+        boxes.append(box.astype(jnp.bfloat16).reshape(experts, -1, model_width))
+    first_box, last_box, probs, slot = lax.optimization_barrier((*boxes, probs, slot))
+
+    early = exchange(first_box)
+    early, last_box = lax.optimization_barrier((early, last_box))
+    late = exchange(last_box)
+    mats = (gate_weight[0], up_weight[0], down_weight[0])
+    out = expert_apply(early, *mats, capacity, 0)
+    out = expert_apply(late, *mats, capacity, EARLY // (capacity - EARLY), out)
+    back = exchange(out)
 
     pick = slot[:, None, :] == wanted[None, :, None]
-    table = table_of(back.reshape(experts, capacity, model_width), cotangent, slot, probs)
+    table = table_of(back, cotangent, slot, probs)
     slot_grad = jnp.sum(jnp.where(pick, table[:, None, :], 0.0), axis=2)
     theirs = exchange(slot_grad[:, None, :])
-    mixed = mixed_of(back.reshape(experts, capacity, model_width), slot, probs)
-    column = column_of(rows.reshape(experts, capacity, model_width), theirs.reshape(experts, capacity))
+    mixed = mixed_of(back, slot, probs)
+    column = column_of(early, late, theirs.reshape(experts, capacity))
     column = column + lax.ppermute(column, "dp", [(0, 1), (1, 0)])
     columns = exchange(jnp.broadcast_to(column.astype(jnp.bfloat16), (experts,) + column.shape))
     columns = columns.reshape(experts, model_width)

time: 419 us -> 410 us (0.979)
  blocking collectives: 328 us -> 283 us
  waiting for transfers between devices: 8.53 us -> 29.5 us
  Pallas kernels: 65.7 us -> 72.5 us
  starting transfers between devices: 5.1 us -> 10.7 us
    all_to_all x3, blocking collectives: 328 us -> 283 us  [exchange(): return lax.all_to_all(rows, GROUP, split_axis=0, concat_axis=0, tiled=True)]
    all_to_all x1 -> x2, waiting for transfers between devices: 7.15 us -> 28.1 us  [exchange(): return lax.all_to_all(rows, GROUP, split_axis=0, concat_axis=0, tiled=True)]
    pallas_call x1 -> x2, Pallas kernels: 44.3 us -> 51 us  [expert_apply(): pl.pallas_call(expert_kernel, out_shape=jax.ShapeDtypeStruct((sources, ca...]
    all_to_all x1 -> x2, starting transfers between devices: 5.02 us -> 10.6 us  [exchange(): return lax.all_to_all(rows, GROUP, split_axis=0, concat_axis=0, tiled=True)]
  transfers between devices with their start and end apart: 2 -> 3, of which waited for: 2 -> 3; matrix products, arithmetic and copies ran while one was open for 0% -> 0% of each run, Pallas kernels for 2% -> 9%
where the time goes in v5:
time: 410 us; the launch traced here: 409 us
  blocking collectives  283 us (69%)
  Pallas kernels  72.5 us (18%)
  waiting for transfers between devices  29.5 us (7%)
  starting transfers between devices  10.7 us (3%)
  matrix products  7.23 us (2%)
    all_to_all x3, blocking collectives, exchange(): return lax.all_to_all(rows, GROUP, split_axis=0, concat_axis=0, tiled=True)  283 us
    pallas_call x2, Pallas kernels, expert_apply(): pl.pallas_call(expert_kernel, out_shape=jax.ShapeDtypeStruct((sources, ca...  51 us
    all_to_all x2, waiting for transfers between devices, exchange(): return lax.all_to_all(rows, GROUP, split_axis=0, concat_axis=0, tiled=True)  28.1 us
    all_to_all x2, starting transfers between devices, exchange(): return lax.all_to_all(rows, GROUP, split_axis=0, concat_axis=0, tiled=True)  10.6 us
    pallas_call x1, Pallas kernels, table_of(): pl.pallas_call(table_kernel, out_shape=jax.ShapeDtypeStruct((experts, row...  8.67 us
  transfers between devices with their start and end apart: 3, of which 3 were waited for; matrix products, arithmetic and copies ran while one was open for 0% of the time, Pallas kernels for 9%

profile of v5, /device:TPU:0, one launch (start us, length us, event | category | flops | bytes accessed | tf_op | source)
XLA Modules:
  0.0 409.0 jit_solution(8195525842393893498)
XLA Ops:
  0.6 0.0 copy-start
  0.7 0.1 slice.7
  0.7 0.8 fusion.3
  1.5 0.1 eq.72
  1.6 0.1 eq.78
  1.7 0.1 fusion.2.slot_ref
  1.9 0.0 copy-done
  1.9 0.0 copy-start.2
  1.9 1.5 fusion.6
  3.4 0.2 bitcast_compare_fusion
  3.6 3.2 fusion
  6.9 2.3 convolution_convert_fusion
  9.2 0.0 copy-done.2
  9.2 0.6 broadcast_divide_fusion.probs_ref
  9.8 112.0 %all_to_all.25.rows_ref.early_hbm = bf16[64,16,4096]{2,1,0:T(8,128)(2,1)} all-to-all(bf16[64,16,4096]{2,1,0:T(8,128)(2,1)S(1)} %bitcast.31), channel_id=1, replica_groups=mesh['dp'=2,'expert'=32,'replica'=2] {'expert','replica'}, dimensions={0} | all-to-all | bytes 16777216 | tf_op jit(solution)/shard_map/all_to_all | solution.py:18
  121.8 5.8 %all-to-all-start.1 = ((bf16[64,8,4096]{2,1,0:T(8,128)(2,1)}), bf16[64,8,4096]{2,1,0:T(8,128)(2,1)}, u32[]{:S(2)}, u32[]{:S(2)}) async-start(bf16[64,8,4096]{2,1,0:T(8,128)(2,1)} %fusion), calls=%async_computation.1 | async-start | bytes 8388608 | tf_op jit(solution)/shard_map/all_to_all | solution.py:18
  127.7 32.2 %experts.2.rest_0_ = bf16[64,24,4096]{2,1,0:T(8,128)(2,1)} custom-call(bf16[64,16,4096]{2,1,0:T(8,128)(2,1)} %all_to_all.25.rows_ref.early_hbm, bf16[4096,768]{1,0:T(8,128)(2,1)} %bitcast.32, bf16[4096,768]{1,0:T(8,128)(2,1)} %bitcast.34, bf16[768,4096]{1,0:T(8,128)(2,1)} %bitcast.36), custom_call_target="tpu_custom_call" | custom-call | flops 19327352832 | bytes 35651584 | tf_op jit(solution)/shard_map/experts/pallas_call | solution.py:64
  159.9 20.8 %all-to-all-done.1.rows_ref.late_hbm = bf16[64,8,4096]{2,1,0:T(8,128)(2,1)} async-done(((bf16[64,8,4096]{2,1,0:T(8,128)(2,1)}), bf16[64,8,4096]{2,1,0:T(8,128)(2,1)}, u32[]{:S(2)}, u32[]{:S(2)}) %all-to-all-start.1) | async-done | bytes 4194336 | tf_op jit(solution)/shard_map/all_to_all | solution.py:18
  180.7 18.8 %experts.3 = bf16[64,24,4096]{2,1,0:T(8,128)(2,1)} custom-call(bf16[64,8,4096]{2,1,0:T(8,128)(2,1)} %all-to-all-done.1.rows_ref.late_hbm, bf16[4096,768]{1,0:T(8,128)(2,1)} %bitcast.33, bf16[4096,768]{1,0:T(8,128)(2,1)} %bitcast.35, bf16[768,4096]{1,0:T(8,128)(2,1)} %bitcast.37, bf16[64,24,4096]{2,1,0:T(8,128)(2,1)} %experts.2.rest_0_), custom_call_target="tpu_custom_call", output_to_operand_aliasing={{}: (4, {})} | custom-call | flops 9663676416 | bytes 27262976 | tf_op jit(solution)/shard_map/experts/pallas_call | solution.py:64
  199.5 152.8 %all_to_all.26.back_ref = bf16[64,24,4096]{2,1,0:T(8,128)(2,1)} all-to-all(bf16[64,24,4096]{2,1,0:T(8,128)(2,1)} %experts.3), channel_id=1, replica_groups=mesh['dp'=2,'expert'=32,'replica'=2] {'expert','replica'}, dimensions={0} | all-to-all | bytes 25165824 | tf_op jit(solution)/shard_map/all_to_all | solution.py:18
  352.3 0.0 copy-start.3
  352.3 8.7 %table.1 = f32[64,128]{1,0:T(8,128)} custom-call(bf16[64,24,4096]{2,1,0:T(8,128)(2,1)} %all_to_all.26.back_ref, bf16[128,4096]{1,0:T(8,128)(2,1)} %cotangent_ref.1, s32[64,128]{1,0:T(8,128)} %copy-done.2, f32[64,128]{1,0:T(8,128)} %broadcast_divide_fusion.probs_ref), custom_call_target="tpu_custom_call" | custom-call | tf_op jit(solution)/shard_map/table/pallas_call | solution.py:182
  360.9 0.0 copy-done.3
  360.9 1.0 select_reduce_fusion
  362.0 17.8 %all_to_all.27 = f32[64,1,24]{2,1,0:T(1,128)} all-to-all(f32[64,1,24]{2,1,0:T(1,128)S(1)} %bitcast.41), channel_id=1, replica_groups=mesh['dp'=2,'expert'=32,'replica'=2] {'expert','replica'}, dimensions={0} | all-to-all | bytes 12288 | tf_op jit(solution)/shard_map/all_to_all | solution.py:18
  379.8 6.4 %column.1 = f32[32,128]{1,0:T(8,128)} custom-call(bf16[64,16,4096]{2,1,0:T(8,128)(2,1)} %all_to_all.25.rows_ref.early_hbm, bf16[64,8,4096]{2,1,0:T(8,128)(2,1)} %all-to-all-done.1.rows_ref.late_hbm, f32[64,24]{1,0:T(8,128)} %bitcast.40), custom_call_target="tpu_custom_call" | custom-call | tf_op jit(solution)/shard_map/column/pallas_call | solution.py:140
  386.2 0.1 collective-permute-start
  386.3 1.4 collective-permute-done
  387.7 0.0 copy-start.1
  387.7 0.8 add_convert_fusion
  388.5 0.9 broadcast_in_dim.43
  389.3 4.8 %all-to-all-start.4 = ((bf16[64,32,128]{2,1,0:T(8,128)(2,1)}), bf16[64,32,128]{2,1,0:T(8,128)(2,1)S(1)}, u32[]{:S(2)}, u32[]{:S(2)}) async-start(bf16[64,32,128]{2,1,0:T(8,128)(2,1)} %broadcast_in_dim.43), calls=%async_computation.4 | async-start | bytes 1048576 | tf_op jit(solution)/shard_map/all_to_all | solution.py:18
  394.1 6.5 %mixed.1 = bf16[128,4096]{1,0:T(8,128)(2,1)} custom-call(bf16[64,24,4096]{2,1,0:T(8,128)(2,1)} %all_to_all.26.back_ref, s32[64,128]{1,0:T(8,128)} %copy-done.2, f32[64,128]{1,0:T(8,128)} %broadcast_divide_fusion.probs_ref), custom_call_target="tpu_custom_call" | custom-call | tf_op jit(solution)/shard_map/mixed/pallas_call | solution.py:218
  400.6 7.3 %all-to-all-done.4 = bf16[64,32,128]{2,1,0:T(8,128)(2,1)S(1)} async-done(((bf16[64,32,128]{2,1,0:T(8,128)(2,1)}), bf16[64,32,128]{2,1,0:T(8,128)(2,1)S(1)}, u32[]{:S(2)}, u32[]{:S(2)}) %all-to-all-start.4) | async-done | bytes 524320 | tf_op jit(solution)/shard_map/all_to_all | solution.py:18
  407.9 1.1 copy.13
  409.0 0.0 copy-done.1
  (4 shorter events, 0.0 us)
Async XLA Ops:
  0.6 1.2 copy-start
  1.9 7.3 %copy-start.2 = (s32[64,128]{1,0:T(8,128)}, s32[64,128]{1,0:T(8,128)S(1)}, u32[]{:S(2)}) copy-start(s32[64,128]{1,0:T(8,128)S(1)} %fusion.2.slot_ref) | copy-start | bytes 98308
  121.8 58.8 %all-to-all-start.1 = ((bf16[64,8,4096]{2,1,0:T(8,128)(2,1)}), bf16[64,8,4096]{2,1,0:T(8,128)(2,1)}, u32[]{:S(2)}, u32[]{:S(2)}) async-start(bf16[64,8,4096]{2,1,0:T(8,128)(2,1)} %fusion), calls=%async_computation.1 | async-start | bytes 8388608 | tf_op jit(solution)/shard_map/all_to_all | solution.py:18
  352.3 8.7 %copy-start.3 = (s32[64,128]{1,0:T(8,128)S(1)}, s32[64,128]{1,0:T(8,128)}, u32[]{:S(2)}) copy-start(s32[64,128]{1,0:T(8,128)} %copy-done.2) | copy-start | bytes 98308
  386.2 1.5 collective-permute-start
  387.7 21.3 %copy-start.1 = (bf16[128,4096]{1,0:T(8,128)(2,1)S(1)}, bf16[128,4096]{1,0:T(8,128)(2,1)}, u32[]{:S(2)}) copy-start(bf16[128,4096]{1,0:T(8,128)(2,1)} %param.7) | copy-start | bytes 3145732
  389.3 18.5 %all-to-all-start.4 = ((bf16[64,32,128]{2,1,0:T(8,128)(2,1)}), bf16[64,32,128]{2,1,0:T(8,128)(2,1)S(1)}, u32[]{:S(2)}, u32[]{:S(2)}) async-start(bf16[64,32,128]{2,1,0:T(8,128)(2,1)} %broadcast_in_dim.43), calls=%async_computation.4 | async-start | bytes 1048576 | tf_op jit(solution)/shard_map/all_to_all | solution.py:18

commit v6 on v5

--- a/solution.py
+++ b/solution.py
@@ -1,3 +1,5 @@
+import functools
+
 import jax
 import jax.numpy as jnp
 from jax import lax
@@ -7,6 +9,7 @@
 
 GROUP = ("expert", "replica")
 EARLY = 16
+STEP = 8
 BLOCKS = 32
 SPAN = 512
 GROUPED = 32
@@ -18,8 +21,9 @@
     return lax.all_to_all(rows, GROUP, split_axis=0, concat_axis=0, tiled=True)
 
 
-def expert_kernel(rows_ref, gate_hbm, up_hbm, down_hbm, *rest):
-    out_ref, gate_mat, up_mat, down_mat, sems = rest[-5:]
+def expert_kernel(held, rows_ref, gate_hbm, up_hbm, down_hbm, *rest):
+    out_refs = rest[held:-4]
+    gate_mat, up_mat, down_mat, sems = rest[-4:]
     copies = [
         pltpu.make_async_copy(source, target, sems.at[n])
         for n, (source, target) in enumerate(
@@ -53,21 +57,26 @@
 
     for start in range(0, width, SPAN):
         part = jnp.dot(hidden, down_mat[:, start : start + SPAN], preferred_element_type=jnp.float32)
-        out_ref[:, :, start : start + SPAN] = part.astype(jnp.bfloat16).reshape(blocks, slots, SPAN)
-
-
-def expert_apply(rows, gate_mat, up_mat, down_mat, capacity, place, into=None):
+        part = part.reshape(blocks, slots, SPAN)
+        for n, out_ref in enumerate(out_refs):
+            out_ref[:, :, start : start + SPAN] = part[:, n * STEP : n * STEP + STEP].astype(jnp.bfloat16)
+
+
+def expert_apply(rows, gate_mat, up_mat, down_mat, outs, into=None):
     sources, slots, width = rows.shape
     depth = gate_mat.shape[1]
     whole = pl.BlockSpec(memory_space=pl.ANY)
     held = [] if into is None else [into]
     return pl.pallas_call(
-        expert_kernel,
-        out_shape=jax.ShapeDtypeStruct((sources, capacity, width), jnp.bfloat16),
+        functools.partial(expert_kernel, len(held)),
+        out_shape=[jax.ShapeDtypeStruct((sources, n, width), jnp.bfloat16) for n, _ in outs],
         grid=(sources // BLOCKS,),
         in_specs=[pl.BlockSpec((BLOCKS, slots, width), lambda i: (i, 0, 0)), whole, whole, whole]
         + [whole] * len(held),
-        out_specs=pl.BlockSpec((BLOCKS, slots, width), lambda i: (i, place, 0)),
+        out_specs=[
+            pl.BlockSpec((BLOCKS, STEP, width), functools.partial(lambda place, i: (i, place, 0), place))
+            for _, place in outs
+        ],
         scratch_shapes=[
             pltpu.VMEM((width, depth), jnp.bfloat16),
             pltpu.VMEM((width, depth), jnp.bfloat16),
@@ -153,21 +162,29 @@
     )(early, late, scales)
 
 
-def table_kernel(back_ref, cotangent_ref, slot_ref, probs_ref, out_ref, dots):
+def picked(slot, start, slots, values):
+    blocks, rows = slot.shape
+    wanted = start + lax.broadcasted_iota(jnp.int32, (blocks, slots, rows), 1)
+    return jnp.where(slot[:, None, :] == wanted, values, 0.0)
+
+
+def table_kernel(early_ref, late_ref, cotangent_ref, slot_ref, probs_ref, out_ref, dots):
     step = pl.program_id(0)
-    blocks, slots, width = back_ref.shape
     rows = cotangent_ref.shape[0]
-    every = lax.dot_general(
-        back_ref[...].reshape(blocks * slots, width),
-        cotangent_ref[...],
-        (((1,), (1,)), ((), ())),
-        preferred_element_type=jnp.float32,
-    ).reshape(blocks, slots, rows)
-    wanted = lax.broadcasted_iota(jnp.int32, (blocks, slots, rows), 1)
-    pick = slot_ref[...][:, None, :] == wanted
-    dots[pl.ds(pl.multiple_of(step * blocks, blocks), blocks), :] = jnp.sum(
-        jnp.where(pick, every, 0.0), axis=1
-    )
+    slot = slot_ref[...]
+    start = 0
+    found = jnp.zeros(slot.shape, jnp.float32)
+    for back_ref in (early_ref, late_ref):
+        blocks, slots, width = back_ref.shape
+        every = lax.dot_general(
+            back_ref[...].reshape(blocks * slots, width),
+            cotangent_ref[...],
+            (((1,), (1,)), ((), ())),
+            preferred_element_type=jnp.float32,
+        ).reshape(blocks, slots, rows)
+        found = found + jnp.sum(picked(slot, start, slots, every), axis=1)
+        start += slots
+    dots[pl.ds(pl.multiple_of(step * GROUPED, GROUPED), GROUPED), :] = found
 
     @pl.when(step == pl.num_programs(0) - 1)
     def _():
@@ -176,15 +193,16 @@
         out_ref[...] = probs * (values - jnp.sum(probs * values, axis=0, keepdims=True))
 
 
-def table_of(back, cotangent, slot, probs):
-    experts, slots, width = back.shape
-    rows = cotangent.shape[0]
+def table_of(early, late, cotangent, slot, probs):
+    experts, rows = slot.shape
+    width = cotangent.shape[1]
     return pl.pallas_call(
         table_kernel,
         out_shape=jax.ShapeDtypeStruct((experts, rows), jnp.float32),
         grid=(experts // GROUPED,),
         in_specs=[
-            pl.BlockSpec((GROUPED, slots, width), lambda i: (i, 0, 0)),
+            pl.BlockSpec((GROUPED, early.shape[1], width), lambda i: (i, 0, 0)),
+            pl.BlockSpec((GROUPED, late.shape[1], width), lambda i: (i, 0, 0)),
             pl.BlockSpec((rows, width), lambda i: (0, 0)),
             pl.BlockSpec((GROUPED, rows), lambda i: (i, 0)),
             pl.BlockSpec((experts, rows), lambda i: (0, 0)),
@@ -193,42 +211,53 @@
         scratch_shapes=[pltpu.VMEM((experts, rows), jnp.float32)],
         compiler_params=pltpu.CompilerParams(vmem_limit_bytes=60 << 20),
         name="table",
-    )(back, cotangent, slot, probs)
-
-
-def mixed_kernel(back_ref, slot_ref, probs_ref, out_ref, share):
-    blocks, slots, width = back_ref.shape
+    )(early, late, cotangent, slot, probs)
+
+
+def mixed_kernel(early_ref, late_ref, slot_ref, probs_ref, out_ref, early_share, late_share):
     rows = out_ref.shape[0]
+    parts = ((early_ref, early_share), (late_ref, late_share))
 
     @pl.when(pl.program_id(0) == 0)
     def _():
-        wanted = lax.broadcasted_iota(jnp.int32, (blocks, slots, rows), 1)
-        pick = slot_ref[...][:, None, :] == wanted
-        chosen = jnp.where(pick, probs_ref[...][:, None, :], 0.0)
-        share[...] = chosen.reshape(blocks * slots, rows).T.astype(jnp.bfloat16)
-
-    out_ref[...] = jnp.dot(
-        share[...], back_ref[...].reshape(blocks * slots, width), preferred_element_type=jnp.float32
-    ).astype(jnp.bfloat16)
-
-
-def mixed_of(back, slot, probs):
-    experts, slots, width = back.shape
-    rows = slot.shape[1]
+        start = 0
+        for back_ref, share in parts:
+            blocks, slots, _ = back_ref.shape
+            chosen = picked(slot_ref[...], start, slots, probs_ref[...][:, None, :])
+            share[...] = chosen.reshape(blocks * slots, rows).T.astype(jnp.bfloat16)
+            start += slots
+
+    total = jnp.zeros(out_ref.shape, jnp.float32)
+    for back_ref, share in parts:
+        blocks, slots, width = back_ref.shape
+        total = total + jnp.dot(
+            share[...], back_ref[...].reshape(blocks * slots, width), preferred_element_type=jnp.float32
+        )
+    out_ref[...] = total.astype(jnp.bfloat16)
+
+
+def mixed_of(early, late, slot, probs):
+    experts, rows = slot.shape
+    width = early.shape[2]
+    tables = pl.BlockSpec((experts, rows), lambda i: (0, 0))
     return pl.pallas_call(
         mixed_kernel,
         out_shape=jax.ShapeDtypeStruct((rows, width), jnp.bfloat16),
         grid=(width // SPANM,),
         in_specs=[
-            pl.BlockSpec((experts, slots, SPANM), lambda i: (0, 0, i)),
-            pl.BlockSpec((experts, rows), lambda i: (0, 0)),
-            pl.BlockSpec((experts, rows), lambda i: (0, 0)),
+            pl.BlockSpec((experts, early.shape[1], SPANM), lambda i: (0, 0, i)),
+            pl.BlockSpec((experts, late.shape[1], SPANM), lambda i: (0, 0, i)),
+            tables,
+            tables,
         ],
         out_specs=pl.BlockSpec((rows, SPANM), lambda i: (0, i)),
-        scratch_shapes=[pltpu.VMEM((rows, experts * slots), jnp.bfloat16)],
+        scratch_shapes=[
+            pltpu.VMEM((rows, experts * early.shape[1]), jnp.bfloat16),
+            pltpu.VMEM((rows, experts * late.shape[1]), jnp.bfloat16),
+        ],
         compiler_params=pltpu.CompilerParams(vmem_limit_bytes=60 << 20),
         name="mixed",
-    )(back, slot, probs)
+    )(early, late, slot, probs)
 
 
 def local(tokens, expert_ids, router_weight, gate_weight, up_weight, down_weight, cotangent):
@@ -244,31 +273,36 @@
     slot = jnp.where(member, before.astype(jnp.int32), -1)
 
     wanted = jnp.arange(capacity, dtype=jnp.int32)
+    boxes = []
+    for numbers in (wanted[:EARLY], wanted[EARLY:]):
+        pick = (slot[:, None, :] == numbers[None, :, None]).reshape(-1, tok_rows)
+        box = jnp.dot(pick.astype(jnp.bfloat16), tokens, preferred_element_type=jnp.float32)
+        boxes.append(box.astype(jnp.bfloat16).reshape(experts, -1, model_width))
+    first_box, last_box, slot = lax.optimization_barrier((*boxes, slot))
+
+    early = exchange(first_box)
+    early, last_box, member, router_weight = lax.optimization_barrier(
+        (early, last_box, member, router_weight)
+    )
+    late = exchange(last_box)
     logits = lax.dot_general(
         router_weight, tokens, (((0,), (1,)), ((), ())), preferred_element_type=jnp.float32
     )
     raised = jnp.where(member, jnp.exp(logits), 0.0)
     probs = raised / jnp.sum(raised, axis=0, keepdims=True)
-    boxes = []
-    for numbers in (wanted[:EARLY], wanted[EARLY:]):
-        pick = (slot[:, None, :] == numbers[None, :, None]).reshape(-1, tok_rows)
-        box = jnp.dot(pick.astype(jnp.bfloat16), tokens, preferred_element_type=jnp.float32)
-        boxes.append(box.astype(jnp.bfloat16).reshape(experts, -1, model_width))
-    first_box, last_box, probs, slot = lax.optimization_barrier((*boxes, probs, slot))
-
-    early = exchange(first_box)
-    early, last_box = lax.optimization_barrier((early, last_box))
-    late = exchange(last_box)
     mats = (gate_weight[0], up_weight[0], down_weight[0])
-    out = expert_apply(early, *mats, capacity, 0)
-    out = expert_apply(late, *mats, capacity, EARLY // (capacity - EARLY), out)
-    back = exchange(out)
-
+    out_early, out_late = expert_apply(early, *mats, ((STEP, 0), (capacity - STEP, 0)))
+    late, out_early = lax.optimization_barrier((late, out_early))
+    back_early = exchange(out_early)
+    (out_late,) = expert_apply(late, *mats, ((capacity - STEP, 1),), out_late)
+    back_early, out_late, probs = lax.optimization_barrier((back_early, out_late, probs))
+    back_late = exchange(out_late)
+
+    table = table_of(back_early, back_late, cotangent, slot, probs)
     pick = slot[:, None, :] == wanted[None, :, None]
-    table = table_of(back, cotangent, slot, probs)
     slot_grad = jnp.sum(jnp.where(pick, table[:, None, :], 0.0), axis=2)
     theirs = exchange(slot_grad[:, None, :])
-    mixed = mixed_of(back, slot, probs)
+    mixed = mixed_of(back_early, back_late, slot, probs)
     column = column_of(early, late, theirs.reshape(experts, capacity))
     column = column + lax.ppermute(column, "dp", [(0, 1), (1, 0)])
     columns = exchange(jnp.broadcast_to(column.astype(jnp.bfloat16), (experts,) + column.shape))

time: 410 us -> 403 us (0.983)
  blocking collectives: 283 us -> 236 us
  waiting for transfers between devices: 29.5 us -> 62.5 us
  starting transfers between devices: 10.7 us -> 18.7 us
    all_to_all x3, blocking collectives: 283 us -> 236 us  [exchange(): return lax.all_to_all(rows, GROUP, split_axis=0, concat_axis=0, tiled=True)]
    all_to_all x2 -> x3, waiting for transfers between devices: 28.1 us -> 61.1 us  [exchange(): return lax.all_to_all(rows, GROUP, split_axis=0, concat_axis=0, tiled=True)]
    all_to_all x2 -> x3, starting transfers between devices: 10.6 us -> 18.6 us  [exchange(): return lax.all_to_all(rows, GROUP, split_axis=0, concat_axis=0, tiled=True)]
  transfers between devices with their start and end apart: 3 -> 4, of which waited for: 3 -> 4; matrix products, arithmetic and copies ran while one was open for 0% -> 0% of each run, Pallas kernels for 9% -> 14%
where the time goes in v6:
time: 403 us; the launch traced here: 402 us
  blocking collectives  236 us (59%)
  Pallas kernels  72.6 us (18%)
  waiting for transfers between devices  62.5 us (16%)
  starting transfers between devices  18.7 us (5%)
  matrix products  6.18 us (2%)
    all_to_all x3, blocking collectives, exchange(): return lax.all_to_all(rows, GROUP, split_axis=0, concat_axis=0, tiled=True)  236 us
    all_to_all x3, waiting for transfers between devices, exchange(): return lax.all_to_all(rows, GROUP, split_axis=0, concat_axis=0, tiled=True)  61.1 us
    pallas_call x2, Pallas kernels, expert_apply(): pl.pallas_call(functools.partial(expert_kernel, len(held)), out_shape=[ja...  51.1 us
    all_to_all x3, starting transfers between devices, exchange(): return lax.all_to_all(rows, GROUP, split_axis=0, concat_axis=0, tiled=True)  18.6 us
    pallas_call x1, Pallas kernels, table_of(): pl.pallas_call(table_kernel, out_shape=jax.ShapeDtypeStruct((experts, row...  8.61 us
  transfers between devices with their start and end apart: 4, of which 4 were waited for; matrix products, arithmetic and copies ran while one was open for 0% of the time, Pallas kernels for 14%

profile of v6, /device:TPU:0, one launch (start us, length us, event | category | flops | bytes accessed | tf_op | source)
XLA Modules:
  0.0 402.1 jit_solution(16833390982607162242)
XLA Ops:
  0.6 0.0 copy-start
  0.7 0.1 slice.7
  0.7 0.8 fusion.3
  1.5 0.1 eq.72
  1.6 0.1 eq.78
  1.7 0.1 fusion.2.slot_ref
  1.9 0.0 copy-start.1
  1.9 0.2 bitcast_compare_fusion
  2.1 0.0 copy-done
  2.1 3.2 fusion
  5.3 2.3 convolution_convert_fusion
  7.6 0.0 copy-done.1
  7.6 112.0 %all_to_all.30.rows_ref.early_hbm = bf16[64,16,4096]{2,1,0:T(8,128)(2,1)} all-to-all(bf16[64,16,4096]{2,1,0:T(8,128)(2,1)S(1)} %bitcast.31), channel_id=1, replica_groups=mesh['dp'=2,'expert'=32,'replica'=2] {'expert','replica'}, dimensions={0} | all-to-all | bytes 16777216 | tf_op jit(solution)/shard_map/all_to_all | solution.py:21
  119.7 5.8 %all-to-all-start.1 = ((bf16[64,8,4096]{2,1,0:T(8,128)(2,1)}), bf16[64,8,4096]{2,1,0:T(8,128)(2,1)}, u32[]{:S(2)}, u32[]{:S(2)}) async-start(bf16[64,8,4096]{2,1,0:T(8,128)(2,1)} %fusion), calls=%async_computation.1 | async-start | bytes 8388608 | tf_op jit(solution)/shard_map/all_to_all | solution.py:21
  125.5 32.3 %experts.2 = (bf16[64,8,4096]{2,1,0:T(8,128)(2,1)}, bf16[64,16,4096]{2,1,0:T(8,128)(2,1)}) custom-call(bf16[64,16,4096]{2,1,0:T(8,128)(2,1)} %all_to_all.30.rows_ref.early_hbm, bf16[4096,768]{1,0:T(8,128)(2,1)} %bitcast.32, bf16[4096,768]{1,0:T(8,128)(2,1)} %bitcast.34, bf16[768,4096]{1,0:T(8,128)(2,1)} %bitcast.36), custom_call_target="tpu_custom_call" | custom-call | flops 19327352832 | bytes 35651584 | tf_op jit(solution)/shard_map/experts/pallas_call | solution.py:70
  157.8 0.0 copy-start.3
  157.8 20.7 %all-to-all-done.1.rows_ref.late_hbm = bf16[64,8,4096]{2,1,0:T(8,128)(2,1)} async-done(((bf16[64,8,4096]{2,1,0:T(8,128)(2,1)}), bf16[64,8,4096]{2,1,0:T(8,128)(2,1)}, u32[]{:S(2)}, u32[]{:S(2)}) %all-to-all-start.1) | async-done | bytes 4194336 | tf_op jit(solution)/shard_map/all_to_all | solution.py:21
  178.5 8.0 %all-to-all-start.2 = ((bf16[64,8,4096]{2,1,0:T(8,128)(2,1)}), bf16[64,8,4096]{2,1,0:T(8,128)(2,1)}, u32[]{:S(2)}, u32[]{:S(2)}) async-start(bf16[64,8,4096]{2,1,0:T(8,128)(2,1)} %get-tuple-element.21), calls=%async_computation.2 | async-start | bytes 8388608 | tf_op jit(solution)/shard_map/all_to_all | solution.py:21
  186.5 0.0 copy-done.3
  186.6 0.5 fusion.6
  187.1 0.6 broadcast_divide_fusion.probs_ref
  187.7 18.8 %experts.3 = bf16[64,16,4096]{2,1,0:T(8,128)(2,1)} custom-call(bf16[64,8,4096]{2,1,0:T(8,128)(2,1)} %all-to-all-done.1.rows_ref.late_hbm, bf16[4096,768]{1,0:T(8,128)(2,1)} %bitcast.33, bf16[4096,768]{1,0:T(8,128)(2,1)} %bitcast.35, bf16[768,4096]{1,0:T(8,128)(2,1)} %bitcast.37, ...), custom_call_target="tpu_custom_call", output_to_operand_aliasing={{}: (4, {})} | custom-call | flops 9663676416 | bytes 27262976 | tf_op jit(solution)/shard_map/experts/pallas_call | solution.py:70
  206.5 33.1 %all-to-all-done.2.early_ref = bf16[64,8,4096]{2,1,0:T(8,128)(2,1)} async-done(((bf16[64,8,4096]{2,1,0:T(8,128)(2,1)}), bf16[64,8,4096]{2,1,0:T(8,128)(2,1)}, u32[]{:S(2)}, u32[]{:S(2)}) %all-to-all-start.2) | async-done | bytes 4194336 | tf_op jit(solution)/shard_map/all_to_all | solution.py:21
  239.7 105.1 %all_to_all.31.late_ref = bf16[64,16,4096]{2,1,0:T(8,128)(2,1)} all-to-all(bf16[64,16,4096]{2,1,0:T(8,128)(2,1)} %experts.3), channel_id=1, replica_groups=mesh['dp'=2,'expert'=32,'replica'=2] {'expert','replica'}, dimensions={0} | all-to-all | bytes 16777216 | tf_op jit(solution)/shard_map/all_to_all | solution.py:21
  344.8 0.0 copy-start.2
  344.8 8.6 %table.1 = f32[64,128]{1,0:T(8,128)} custom-call(bf16[64,8,4096]{2,1,0:T(8,128)(2,1)} %all-to-all-done.2.early_ref, bf16[64,16,4096]{2,1,0:T(8,128)(2,1)} %all_to_all.31.late_ref, bf16[128,4096]{1,0:T(8,128)(2,1)} %cotangent_ref.1, s32[64,128]{1,0:T(8,128)} %copy-done.1, f32[64,128]{1,0:T(8,128)} %broadcast_divide_fusion.probs_ref), custom_call_target="tpu_custom_call" | custom-call | tf_op jit(solution)/shard_map/table/pallas_call | solution.py:199
  353.4 0.0 copy-done.2
  353.4 1.0 select_reduce_fusion
  354.4 18.6 %all_to_all.32 = f32[64,1,24]{2,1,0:T(1,128)} all-to-all(f32[64,1,24]{2,1,0:T(1,128)S(1)} %bitcast.41), channel_id=1, replica_groups=mesh['dp'=2,'expert'=32,'replica'=2] {'expert','replica'}, dimensions={0} | all-to-all | bytes 12288 | tf_op jit(solution)/shard_map/all_to_all | solution.py:21
  373.0 6.4 %column.1 = f32[32,128]{1,0:T(8,128)} custom-call(bf16[64,16,4096]{2,1,0:T(8,128)(2,1)} %all_to_all.30.rows_ref.early_hbm, bf16[64,8,4096]{2,1,0:T(8,128)(2,1)} %all-to-all-done.1.rows_ref.late_hbm, f32[64,24]{1,0:T(8,128)} %bitcast.40), custom_call_target="tpu_custom_call" | custom-call | tf_op jit(solution)/shard_map/column/pallas_call | solution.py:149
  379.4 0.1 collective-permute-start
  379.5 1.4 collective-permute-done
  380.9 0.7 add_convert_fusion
  381.6 0.9 broadcast_in_dim.43
  382.5 4.8 %all-to-all-start.5 = ((bf16[64,32,128]{2,1,0:T(8,128)(2,1)}), bf16[64,32,128]{2,1,0:T(8,128)(2,1)S(1)}, u32[]{:S(2)}, u32[]{:S(2)}) async-start(bf16[64,32,128]{2,1,0:T(8,128)(2,1)} %broadcast_in_dim.43), calls=%async_computation.5 | async-start | bytes 1048576 | tf_op jit(solution)/shard_map/all_to_all | solution.py:21
  387.2 6.5 %mixed.1 = bf16[128,4096]{1,0:T(8,128)(2,1)} custom-call(bf16[64,8,4096]{2,1,0:T(8,128)(2,1)} %all-to-all-done.2.early_ref, bf16[64,16,4096]{2,1,0:T(8,128)(2,1)} %all_to_all.31.late_ref, s32[64,128]{1,0:T(8,128)} %copy-done.1, f32[64,128]{1,0:T(8,128)} %broadcast_divide_fusion.probs_ref), custom_call_target="tpu_custom_call" | custom-call | tf_op jit(solution)/shard_map/mixed/pallas_call | solution.py:243
  393.7 7.3 %all-to-all-done.5 = bf16[64,32,128]{2,1,0:T(8,128)(2,1)S(1)} async-done(((bf16[64,32,128]{2,1,0:T(8,128)(2,1)}), bf16[64,32,128]{2,1,0:T(8,128)(2,1)S(1)}, u32[]{:S(2)}, u32[]{:S(2)}) %all-to-all-start.5) | async-done | bytes 524320 | tf_op jit(solution)/shard_map/all_to_all | solution.py:21
  401.0 1.1 copy.13
  (4 shorter events, 0.0 us)
Async XLA Ops:
  0.6 1.5 copy-start
  1.9 5.8 %copy-start.1 = (s32[64,128]{1,0:T(8,128)}, s32[64,128]{1,0:T(8,128)S(1)}, u32[]{:S(2)}) copy-start(s32[64,128]{1,0:T(8,128)S(1)} %fusion.2.slot_ref) | copy-start | bytes 98308
  119.7 58.9 %all-to-all-start.1 = ((bf16[64,8,4096]{2,1,0:T(8,128)(2,1)}), bf16[64,8,4096]{2,1,0:T(8,128)(2,1)}, u32[]{:S(2)}, u32[]{:S(2)}) async-start(bf16[64,8,4096]{2,1,0:T(8,128)(2,1)} %fusion), calls=%async_computation.1 | async-start | bytes 8388608 | tf_op jit(solution)/shard_map/all_to_all | solution.py:21
  157.8 28.7 %copy-start.3 = (bf16[4096,64]{0,1:T(8,128)(2,1)S(1)}, bf16[4096,64]{0,1:T(8,128)(2,1)}, u32[]{:S(2)}) copy-start(bf16[4096,64]{0,1:T(8,128)(2,1)} %param.9) | copy-start | bytes 1572868
  178.5 61.2 %all-to-all-start.2 = ((bf16[64,8,4096]{2,1,0:T(8,128)(2,1)}), bf16[64,8,4096]{2,1,0:T(8,128)(2,1)}, u32[]{:S(2)}, u32[]{:S(2)}) async-start(bf16[64,8,4096]{2,1,0:T(8,128)(2,1)} %get-tuple-element.21), calls=%async_computation.2 | async-start | bytes 8388608 | tf_op jit(solution)/shard_map/all_to_all | solution.py:21
  344.8 8.6 %copy-start.2 = (s32[64,128]{1,0:T(8,128)S(1)}, s32[64,128]{1,0:T(8,128)}, u32[]{:S(2)}) copy-start(s32[64,128]{1,0:T(8,128)} %copy-done.1) | copy-start | bytes 98308
  379.4 1.5 collective-permute-start
  382.5 18.5 %all-to-all-start.5 = ((bf16[64,32,128]{2,1,0:T(8,128)(2,1)}), bf16[64,32,128]{2,1,0:T(8,128)(2,1)S(1)}, u32[]{:S(2)}, u32[]{:S(2)}) async-start(bf16[64,32,128]{2,1,0:T(8,128)(2,1)} %broadcast_in_dim.43), calls=%async_computation.5 | async-start | bytes 1048576 | tf_op jit(solution)/shard_map/all_to_all | solution.py:21

commit v7 on v6

--- a/solution.py
+++ b/solution.py
@@ -12,7 +12,7 @@
 STEP = 8
 BLOCKS = 32
 SPAN = 512
-GROUPED = 32
+SPANT = 1024
 PIECES = 16
 SPANM = 2048
 
@@ -168,49 +168,54 @@
     return jnp.where(slot[:, None, :] == wanted, values, 0.0)
 
 
-def table_kernel(early_ref, late_ref, cotangent_ref, slot_ref, probs_ref, out_ref, dots):
+def slot_grad_kernel(early_ref, late_ref, cotangent_ref, slot_ref, probs_ref, out_ref, early, late):
     step = pl.program_id(0)
-    rows = cotangent_ref.shape[0]
-    slot = slot_ref[...]
-    start = 0
-    found = jnp.zeros(slot.shape, jnp.float32)
-    for back_ref in (early_ref, late_ref):
+    parts = ((early_ref, early), (late_ref, late))
+
+    @pl.when(step == 0)
+    def _():
+        for _, total in parts:
+            total[...] = jnp.zeros_like(total)
+
+    for back_ref, total in parts:
         blocks, slots, width = back_ref.shape
-        every = lax.dot_general(
+        total[...] += lax.dot_general(
             back_ref[...].reshape(blocks * slots, width),
             cotangent_ref[...],
             (((1,), (1,)), ((), ())),
             preferred_element_type=jnp.float32,
-        ).reshape(blocks, slots, rows)
-        found = found + jnp.sum(picked(slot, start, slots, every), axis=1)
-        start += slots
-    dots[pl.ds(pl.multiple_of(step * GROUPED, GROUPED), GROUPED), :] = found
+        )
 
     @pl.when(step == pl.num_programs(0) - 1)
     def _():
+        slot = slot_ref[...]
         probs = probs_ref[...]
-        values = dots[...]
-        out_ref[...] = probs * (values - jnp.sum(probs * values, axis=0, keepdims=True))
-
-
-def table_of(early, late, cotangent, slot, probs):
+        dots = jnp.zeros(slot.shape, jnp.float32)
+        start = 0
+        for back_ref, total in parts:
+            blocks, slots, _ = back_ref.shape
+            every = total[...].reshape(blocks, slots, slot.shape[1])
+            dots = dots + jnp.sum(picked(slot, start, slots, every), axis=1)
+            start += slots
+        table = probs * (dots - jnp.sum(probs * dots, axis=0, keepdims=True))
+        out_ref[...] = jnp.sum(picked(slot, 0, start, table[:, None, :]), axis=2)
+
+
+def slot_grad_of(early, late, cotangent, slot, probs):
     experts, rows = slot.shape
+    counts = (early.shape[1], late.shape[1])
     width = cotangent.shape[1]
+    tables = pl.BlockSpec((experts, rows), lambda i: (0, 0))
     return pl.pallas_call(
-        table_kernel,
-        out_shape=jax.ShapeDtypeStruct((experts, rows), jnp.float32),
-        grid=(experts // GROUPED,),
-        in_specs=[
-            pl.BlockSpec((GROUPED, early.shape[1], width), lambda i: (i, 0, 0)),
-            pl.BlockSpec((GROUPED, late.shape[1], width), lambda i: (i, 0, 0)),
-            pl.BlockSpec((rows, width), lambda i: (0, 0)),
-            pl.BlockSpec((GROUPED, rows), lambda i: (i, 0)),
-            pl.BlockSpec((experts, rows), lambda i: (0, 0)),
-        ],
-        out_specs=pl.BlockSpec((experts, rows), lambda i: (0, 0)),
-        scratch_shapes=[pltpu.VMEM((experts, rows), jnp.float32)],
+        slot_grad_kernel,
+        out_shape=jax.ShapeDtypeStruct((experts, sum(counts)), jnp.float32),
+        grid=(width // SPANT,),
+        in_specs=[pl.BlockSpec((experts, n, SPANT), lambda i: (0, 0, i)) for n in counts]
+        + [pl.BlockSpec((rows, SPANT), lambda i: (0, i)), tables, tables],
+        out_specs=pl.BlockSpec((experts, sum(counts)), lambda i: (0, 0)),
+        scratch_shapes=[pltpu.VMEM((experts * n, rows), jnp.float32) for n in counts],
         compiler_params=pltpu.CompilerParams(vmem_limit_bytes=60 << 20),
-        name="table",
+        name="slot_grad",
     )(early, late, cotangent, slot, probs)
 
 
@@ -298,9 +303,7 @@
     back_early, out_late, probs = lax.optimization_barrier((back_early, out_late, probs))
     back_late = exchange(out_late)
 
-    table = table_of(back_early, back_late, cotangent, slot, probs)
-    pick = slot[:, None, :] == wanted[None, :, None]
-    slot_grad = jnp.sum(jnp.where(pick, table[:, None, :], 0.0), axis=2)
+    slot_grad = slot_grad_of(back_early, back_late, cotangent, slot, probs)
     theirs = exchange(slot_grad[:, None, :])
     mixed = mixed_of(back_early, back_late, slot, probs)
     column = column_of(early, late, theirs.reshape(experts, capacity))

time: 403 us -> 402 us (level)
  no operation moved by 1% of the time
where the time goes in v7:
time: 402 us; the launch traced here: 401 us
  blocking collectives  236 us (59%)
  Pallas kernels  72.8 us (18%)
  waiting for transfers between devices  62.4 us (16%)
  starting transfers between devices  18.8 us (5%)
  matrix products  6.19 us (2%)
    all_to_all x3, blocking collectives, exchange(): return lax.all_to_all(rows, GROUP, split_axis=0, concat_axis=0, tiled=True)  236 us
    all_to_all x3, waiting for transfers between devices, exchange(): return lax.all_to_all(rows, GROUP, split_axis=0, concat_axis=0, tiled=True)  61 us
    pallas_call x2, Pallas kernels, expert_apply(): pl.pallas_call(functools.partial(expert_kernel, len(held)), out_shape=[ja...  51.1 us
    all_to_all x3, starting transfers between devices, exchange(): return lax.all_to_all(rows, GROUP, split_axis=0, concat_axis=0, tiled=True)  18.7 us
    pallas_call x1, Pallas kernels, slot_grad_of(): pl.pallas_call(slot_grad_kernel, out_shape=jax.ShapeDtypeStruct((experts,...  8.83 us
  transfers between devices with their start and end apart: 4, of which 4 were waited for; matrix products, arithmetic and copies ran while one was open for 0% of the time, Pallas kernels for 14%

profile of v7, /device:TPU:0, one launch (start us, length us, event | category | flops | bytes accessed | tf_op | source)
XLA Modules:
  0.0 401.4 jit_solution(9968979209751501306)
XLA Ops:
  0.6 0.0 copy-start
  0.7 0.1 slice.7
  0.7 0.8 fusion.3
  1.5 0.1 eq.59
  1.6 0.1 eq.65
  1.7 0.1 fusion.2.slot_ref
  1.9 0.0 copy-start.1
  1.9 0.2 bitcast_compare_fusion
  2.1 0.0 copy-done
  2.1 3.2 fusion
  5.3 2.3 convolution_convert_fusion
  7.6 0.0 copy-done.1
  7.7 112.0 %all_to_all.30.rows_ref.early_hbm = bf16[64,16,4096]{2,1,0:T(8,128)(2,1)} all-to-all(bf16[64,16,4096]{2,1,0:T(8,128)(2,1)S(1)} %bitcast.31), channel_id=1, replica_groups=mesh['dp'=2,'expert'=32,'replica'=2] {'expert','replica'}, dimensions={0} | all-to-all | bytes 16777216 | tf_op jit(solution)/shard_map/all_to_all | solution.py:21
  119.7 5.9 %all-to-all-start.1 = ((bf16[64,8,4096]{2,1,0:T(8,128)(2,1)}), bf16[64,8,4096]{2,1,0:T(8,128)(2,1)}, u32[]{:S(2)}, u32[]{:S(2)}) async-start(bf16[64,8,4096]{2,1,0:T(8,128)(2,1)} %fusion), calls=%async_computation.1 | async-start | bytes 8388608 | tf_op jit(solution)/shard_map/all_to_all | solution.py:21
  125.5 32.3 %experts.2 = (bf16[64,8,4096]{2,1,0:T(8,128)(2,1)}, bf16[64,16,4096]{2,1,0:T(8,128)(2,1)}) custom-call(bf16[64,16,4096]{2,1,0:T(8,128)(2,1)} %all_to_all.30.rows_ref.early_hbm, bf16[4096,768]{1,0:T(8,128)(2,1)} %bitcast.32, bf16[4096,768]{1,0:T(8,128)(2,1)} %bitcast.34, bf16[768,4096]{1,0:T(8,128)(2,1)} %bitcast.36), custom_call_target="tpu_custom_call" | custom-call | flops 19327352832 | bytes 35651584 | tf_op jit(solution)/shard_map/experts/pallas_call | solution.py:70
  157.8 0.0 copy-start.2
  157.8 20.7 %all-to-all-done.1.rows_ref.late_hbm = bf16[64,8,4096]{2,1,0:T(8,128)(2,1)} async-done(((bf16[64,8,4096]{2,1,0:T(8,128)(2,1)}), bf16[64,8,4096]{2,1,0:T(8,128)(2,1)}, u32[]{:S(2)}, u32[]{:S(2)}) %all-to-all-start.1) | async-done | bytes 4194336 | tf_op jit(solution)/shard_map/all_to_all | solution.py:21
  178.5 8.0 %all-to-all-start.2 = ((bf16[64,8,4096]{2,1,0:T(8,128)(2,1)}), bf16[64,8,4096]{2,1,0:T(8,128)(2,1)}, u32[]{:S(2)}, u32[]{:S(2)}) async-start(bf16[64,8,4096]{2,1,0:T(8,128)(2,1)} %get-tuple-element.21), calls=%async_computation.2 | async-start | bytes 8388608 | tf_op jit(solution)/shard_map/all_to_all | solution.py:21
  186.5 0.0 copy-done.2
  186.6 0.5 fusion.6
  187.1 0.6 broadcast_divide_fusion.probs_ref
  187.7 18.9 %experts.3 = bf16[64,16,4096]{2,1,0:T(8,128)(2,1)} custom-call(bf16[64,8,4096]{2,1,0:T(8,128)(2,1)} %all-to-all-done.1.rows_ref.late_hbm, bf16[4096,768]{1,0:T(8,128)(2,1)} %bitcast.33, bf16[4096,768]{1,0:T(8,128)(2,1)} %bitcast.35, bf16[768,4096]{1,0:T(8,128)(2,1)} %bitcast.37, ...), custom_call_target="tpu_custom_call", output_to_operand_aliasing={{}: (4, {})} | custom-call | flops 9663676416 | bytes 27262976 | tf_op jit(solution)/shard_map/experts/pallas_call | solution.py:70
  206.5 33.1 %all-to-all-done.2.early_ref = bf16[64,8,4096]{2,1,0:T(8,128)(2,1)} async-done(((bf16[64,8,4096]{2,1,0:T(8,128)(2,1)}), bf16[64,8,4096]{2,1,0:T(8,128)(2,1)}, u32[]{:S(2)}, u32[]{:S(2)}) %all-to-all-start.2) | async-done | bytes 4194336 | tf_op jit(solution)/shard_map/all_to_all | solution.py:21
  239.7 105.1 %all_to_all.31.late_ref = bf16[64,16,4096]{2,1,0:T(8,128)(2,1)} all-to-all(bf16[64,16,4096]{2,1,0:T(8,128)(2,1)} %experts.3), channel_id=1, replica_groups=mesh['dp'=2,'expert'=32,'replica'=2] {'expert','replica'}, dimensions={0} | all-to-all | bytes 16777216 | tf_op jit(solution)/shard_map/all_to_all | solution.py:21
  344.8 8.8 %slot_grad.1 = f32[64,24]{1,0:T(8,128)} custom-call(bf16[64,8,4096]{2,1,0:T(8,128)(2,1)} %all-to-all-done.2.early_ref, bf16[64,16,4096]{2,1,0:T(8,128)(2,1)} %all_to_all.31.late_ref, bf16[128,4096]{1,0:T(8,128)(2,1)} %cotangent_ref.1, s32[64,128]{1,0:T(8,128)} %copy-done.1, f32[64,128]{1,0:T(8,128)} %broadcast_divide_fusion.probs_ref), custom_call_target="tpu_custom_call" | custom-call | tf_op jit(solution)/shard_map/slot_grad/pallas_call | solution.py:209
  353.6 18.7 %all_to_all.32 = f32[64,1,24]{2,1,0:T(1,128)} all-to-all(f32[64,1,24]{2,1,0:T(1,128)} %bitcast.41), channel_id=1, replica_groups=mesh['dp'=2,'expert'=32,'replica'=2] {'expert','replica'}, dimensions={0} | all-to-all | bytes 12288 | tf_op jit(solution)/shard_map/all_to_all | solution.py:21
  372.3 6.4 %column.1 = f32[32,128]{1,0:T(8,128)} custom-call(bf16[64,16,4096]{2,1,0:T(8,128)(2,1)} %all_to_all.30.rows_ref.early_hbm, bf16[64,8,4096]{2,1,0:T(8,128)(2,1)} %all-to-all-done.1.rows_ref.late_hbm, f32[64,24]{1,0:T(8,128)} %bitcast.40), custom_call_target="tpu_custom_call" | custom-call | tf_op jit(solution)/shard_map/column/pallas_call | solution.py:149
  378.7 0.1 collective-permute-start
  378.8 1.4 collective-permute-done
  380.2 0.7 add_convert_fusion
  380.9 0.9 broadcast_in_dim.26
  381.8 4.9 %all-to-all-start.5 = ((bf16[64,32,128]{2,1,0:T(8,128)(2,1)}), bf16[64,32,128]{2,1,0:T(8,128)(2,1)S(1)}, u32[]{:S(2)}, u32[]{:S(2)}) async-start(bf16[64,32,128]{2,1,0:T(8,128)(2,1)} %broadcast_in_dim.26), calls=%async_computation.5 | async-start | bytes 1048576 | tf_op jit(solution)/shard_map/all_to_all | solution.py:21
  386.6 6.5 %mixed.1 = bf16[128,4096]{1,0:T(8,128)(2,1)} custom-call(bf16[64,8,4096]{2,1,0:T(8,128)(2,1)} %all-to-all-done.2.early_ref, bf16[64,16,4096]{2,1,0:T(8,128)(2,1)} %all_to_all.31.late_ref, s32[64,128]{1,0:T(8,128)} %copy-done.1, f32[64,128]{1,0:T(8,128)} %broadcast_divide_fusion.probs_ref), custom_call_target="tpu_custom_call" | custom-call | tf_op jit(solution)/shard_map/mixed/pallas_call | solution.py:248
  393.1 7.2 %all-to-all-done.5 = bf16[64,32,128]{2,1,0:T(8,128)(2,1)S(1)} async-done(((bf16[64,32,128]{2,1,0:T(8,128)(2,1)}), bf16[64,32,128]{2,1,0:T(8,128)(2,1)S(1)}, u32[]{:S(2)}, u32[]{:S(2)}) %all-to-all-start.5) | async-done | bytes 524320 | tf_op jit(solution)/shard_map/all_to_all | solution.py:21
  400.3 1.1 copy.14
  (4 shorter events, 0.0 us)
Async XLA Ops:
  0.6 1.5 copy-start
  1.9 5.8 %copy-start.1 = (s32[64,128]{1,0:T(8,128)}, s32[64,128]{1,0:T(8,128)S(1)}, u32[]{:S(2)}) copy-start(s32[64,128]{1,0:T(8,128)S(1)} %fusion.2.slot_ref) | copy-start | bytes 98308
  119.7 58.9 %all-to-all-start.1 = ((bf16[64,8,4096]{2,1,0:T(8,128)(2,1)}), bf16[64,8,4096]{2,1,0:T(8,128)(2,1)}, u32[]{:S(2)}, u32[]{:S(2)}) async-start(bf16[64,8,4096]{2,1,0:T(8,128)(2,1)} %fusion), calls=%async_computation.1 | async-start | bytes 8388608 | tf_op jit(solution)/shard_map/all_to_all | solution.py:21
  157.8 28.8 %copy-start.2 = (bf16[4096,64]{0,1:T(8,128)(2,1)S(1)}, bf16[4096,64]{0,1:T(8,128)(2,1)}, u32[]{:S(2)}) copy-start(bf16[4096,64]{0,1:T(8,128)(2,1)} %param.9) | copy-start | bytes 1572868
  178.5 61.2 %all-to-all-start.2 = ((bf16[64,8,4096]{2,1,0:T(8,128)(2,1)}), bf16[64,8,4096]{2,1,0:T(8,128)(2,1)}, u32[]{:S(2)}, u32[]{:S(2)}) async-start(bf16[64,8,4096]{2,1,0:T(8,128)(2,1)} %get-tuple-element.21), calls=%async_computation.2 | async-start | bytes 8388608 | tf_op jit(solution)/shard_map/all_to_all | solution.py:21
  378.7 1.5 collective-permute-start
  381.8 18.5 %all-to-all-start.5 = ((bf16[64,32,128]{2,1,0:T(8,128)(2,1)}), bf16[64,32,128]{2,1,0:T(8,128)(2,1)S(1)}, u32[]{:S(2)}, u32[]{:S(2)}) async-start(bf16[64,32,128]{2,1,0:T(8,128)(2,1)} %broadcast_in_dim.26), calls=%async_computation.5 | async-start | bytes 1048576 | tf_op jit(solution)/shard_map/all_to_all | solution.py:21
